TPU v7x, 256 devices: a whole 4x4x8 slice. The times are simulated.
256 devices in a mesh: vocab: 32 (over x, z), prange: 4 (over y), query: 2 (over core).
Axes of the slice: x: 4, y: 4, z: 8, core: 2. Of those that a mesh axis runs over, the one named last changes fastest.
Arguments:
- term_ids: int32 [4096, 32], P('query'), may hold values from 0 to 32767
- term_weights: bfloat16 [4096, 32], P('query'), may hold values from 0.049804688 to 1
- impact: bfloat16 [32768, 8192], P('vocab', 'prange'), may hold values from 0.0099487305 to 1
- query_rows: bfloat16 [128, 32768], P(('prange', 'query'), 'vocab'), may hold values from -0.3125 to 0.3125
- candidates: int32 [128, 4], P(('prange', 'query')), may hold values from 0 to 63, all different within a row; in each aligned block of 16 rows (0 to 15, 16 to 31, ...) at most 2 rows name the same one
Outputs:
- first_scores: bfloat16 [4, 2048, 4096], P('prange', 'vocab', 'query')
- rescored: float32 [128, 4, 128], P(('prange', 'query'), None, 'vocab')
Inputs may be any that keep to these rules, and one draw needn't show every extreme that they name: `candidates`: each row names 4 different blocks. The 16 rows held by one device name any block at most 2 times, and some block exactly 2 times.
All inputs are finite; a program needn't handle non-finite values.
Results may differ from a plain program's by a relative error of at most 0.019.
Values may be sent and summed in bfloat16 or wider, within the bound.
No kernel may reach another device: no remote copies, remote signals or barrier semaphores. Data moves between devices by JAX's collectives and lax.ppermute only.
A program may use at most 64 MiB of HBM per device.

v0:
```python
import functools

import jax
import jax.numpy as jnp
from jax import lax
from jax.experimental import pallas as pl
from jax.experimental.pallas import tpu as pltpu
from jax.sharding import Mesh
from jax.sharding import PartitionSpec as P


BLOCK = 128
CANDS = 4
NX = 4
NZ = 8
NY = 4
LANES = 128
GROUP = 8
FIRST = 256
CHUNKS = 2
UNROLL = 32
CUTS = 4
F32 = jnp.float32
BF16 = jnp.bfloat16


def shifted(array, axis, shift):
    size = lax.axis_size(axis)
    return lax.ppermute(array, axis, [(i, (i + shift) % size) for i in range(size)])


def kept_in_hbm(array):
    return pltpu.with_memory_space_constraint(array, pltpu.HBM)


def dense_kernel(pos_ref, ids_ref, weights_ref, dense_ref, turned_ref, low_ref, key_ref, weight_ref):
    x, z, core = pos_ref[0], pos_ref[1], pos_ref[2]
    terms, _ = ids_ref.shape
    groups, pairs = low_ref.shape
    highs = dense_ref.shape[1] // FIRST
    ids = ids_ref[...]
    x_rel = ((ids >> 13) - x) & (NX - 1)
    half_rel = ((ids >> 9) & 1) ^ core
    high = x_rel * 4 + half_rel * 2 + ((ids >> 8) & 1)
    key = high * GROUP + (lax.broadcasted_iota(jnp.int32, ids.shape, 1) & (GROUP - 1))
    key = jnp.where(((ids >> 10) & (NZ - 1)) == z, key, -1)
    low = (ids & (FIRST - 1)).astype(F32)
    weights = weights_ref[...].astype(F32)
    turned_ref[...] = jnp.concatenate([low, key.astype(F32), weights, weights], axis=0).T
    place = lax.broadcasted_iota(jnp.int32, (groups, LANES), 1) // terms
    across = LANES // terms
    for kind, to_ref in enumerate((low_ref, key_ref, weight_ref)):
        for side in range(pairs // LANES):
            row = None
            for j in range(across):
                part = turned_ref[pl.ds(side * across + j, groups, stride=GROUP), :]
                shift = (terms * (j - kind)) % LANES
                part = pltpu.roll(part, shift, 1) if shift else part
                row = part if row is None else jnp.where(place == j, part, row)
            to_ref[:, side * LANES : (side + 1) * LANES] = row
    low_rows = lax.broadcasted_iota(jnp.int32, (FIRST, pairs), 0).astype(F32).astype(BF16)
    key_rows = lax.broadcasted_iota(jnp.int32, (highs * GROUP, pairs), 0).astype(F32).astype(BF16)
    one = jnp.ones((), BF16)
    zero = jnp.zeros((), BF16)

    def one_group(g):
        low = low_ref[pl.ds(g, 1), :].astype(BF16)
        keys = key_ref[pl.ds(g, 1), :].astype(BF16)
        weights = weight_ref[pl.ds(g, 1), :].astype(BF16)
        ones = jnp.where(low_rows == low, one, zero)
        spread = jnp.where(key_rows == keys, weights, zero)
        made = lax.dot_general(spread, ones, (((1,), (1,)), ((), ())), preferred_element_type=F32)
        return made.reshape(highs, GROUP, FIRST)

    def pair_of_groups(i, carry):
        both = jnp.concatenate([one_group(2 * i), one_group(2 * i + 1)], axis=1).astype(BF16)
        row = pl.multiple_of(i * 2 * GROUP, 2 * GROUP)
        for h in range(highs):
            dense_ref[pl.ds(row, 2 * GROUP), h * FIRST : (h + 1) * FIRST] = both[h]
        return carry

    lax.fori_loop(0, groups // 2, pair_of_groups, 0, unroll=UNROLL)


def build_dense(place, ids, weights, width, chunk):
    blocks = 2
    terms = ids.shape[0]
    queries = ids.shape[1] // CHUNKS // blocks
    groups = queries // GROUP
    spec = pl.BlockSpec((terms, queries), lambda i, s: (0, chunk * blocks + i))
    rows = pltpu.VMEM((groups, GROUP * terms), F32)
    return pl.pallas_call(
        dense_kernel,
        out_shape=pltpu.HBM((queries * blocks, width), BF16),
        grid_spec=pltpu.PrefetchScalarGridSpec(
            num_scalar_prefetch=1,
            grid=(blocks,),
            in_specs=[spec, spec],
            out_specs=pl.BlockSpec((queries, width), lambda i, s: (i, 0)),
            scratch_shapes=[pltpu.VMEM((queries, LANES), F32), rows, rows, rows],
        ),
        compiler_params=pltpu.CompilerParams(vmem_limit_bytes=12 << 20),
        cost_estimate=pl.CostEstimate(flops=10**10, transcendentals=0, bytes_accessed=queries * blocks * width * 2),
        name="dense_build",
    )(place, kept_in_hbm(ids), kept_in_hbm(weights))


def rows_kernel(pos_ref, r0, r1, r2, r3, impact_ref, o0, o1, o2, o3):
    y = pos_ref[3]
    width = impact_ref.shape[0]
    full = r0.shape[0]
    rows = jnp.concatenate([r[:, :width] for r in (r0, r1, r2, r3)], axis=0)
    scores = jnp.dot(rows, impact_ref[...], preferred_element_type=F32)
    blocks = impact_ref.shape[1] // BLOCK
    for home, (r, o) in enumerate(((r0, o0), (r1, o1), (r2, o2), (r3, o3))):
        named = r[:, width : width + LANES].astype(F32).astype(jnp.int32) - y * blocks
        mine = scores[home * full : (home + 1) * full]
        for c in range(CANDS):
            column = named[:, c : c + 1]
            picked = jnp.zeros((full, BLOCK), F32)
            for b in range(blocks):
                picked = jnp.where(column == b, mine[:, b * BLOCK : (b + 1) * BLOCK], picked)
            o[c * full : (c + 1) * full, :] = picked.astype(BF16)


def score_rows(place, gathered, impact):
    full = gathered[0].shape[0]
    one = jax.ShapeDtypeStruct((full * CANDS, BLOCK), BF16)
    vmem = pl.BlockSpec(memory_space=pltpu.VMEM)
    return pl.pallas_call(
        rows_kernel,
        out_shape=[one] * NY,
        in_specs=[pl.BlockSpec(memory_space=pltpu.SMEM)] + [vmem] * 5,
        out_specs=[vmem] * NY,
        compiler_params=pltpu.CompilerParams(vmem_limit_bytes=8 << 20),
        cost_estimate=pl.CostEstimate(flops=2 * 10**9, transcendentals=0, bytes_accessed=4 << 20),
        name="score_rows",
    )(place, *gathered, impact)


def score_kernel(pos_ref, dense_ref, *refs, extra):
    piece_refs = refs[:8]
    extra_refs = refs[8:12] if extra else ()
    out_refs = refs[-NZ - 1 : -1]
    made_ref = refs[-1]
    z = pos_ref[1]
    rows, _ = dense_ref.shape[1:]
    depth = piece_refs[0].shape[0]
    chunk = made_ref.shape[1]
    half = LANES // 2
    step = pl.program_id(0)
    last = step == pl.num_programs(0) - 1
    made = []
    for part in range(2):
        total = None
        for i, piece in enumerate(piece_refs):
            block = dense_ref[part, :, i * depth : (i + 1) * depth]
            one = jnp.dot(block, piece[...], preferred_element_type=F32)
            total = one if total is None else total + one
        made.append(total)
    left = lax.broadcasted_iota(jnp.int32, (rows, LANES), 1) < half
    at = pl.ds(pl.multiple_of(step * rows, rows), rows)
    for m in range(NZ // 2):
        a = made[0][:, m * LANES : (m + 1) * LANES]
        b = made[1][:, m * LANES : (m + 1) * LANES]
        made_ref[2 * m, at, :] = jnp.where(left, a, pltpu.roll(b, half, 1)).astype(BF16)
        made_ref[2 * m + 1, at, :] = jnp.where(left, pltpu.roll(a, half, 1), b).astype(BF16)

    @pl.when(last)
    def _():
        for j, out_ref in enumerate(out_refs):
            out_ref[:chunk, :] = made_ref[(z + j) & (NZ - 1)]
        if extra:
            pack_rows(z, chunk, extra_refs, out_refs)


def pack_rows(z, chunk, extra_refs, out_refs):
    total = extra_refs[0][...].astype(F32)
    for r in extra_refs[1:]:
        total = total + r[...].astype(F32)
    wide, own = LANES // NX, LANES // (NX * NZ)
    deep = total.shape[0] // NZ
    place = (lax.broadcasted_iota(jnp.int32, (deep, LANES), 1) & (wide - 1)) // own
    for j, out_ref in enumerate(out_refs):
        to_z = (z + j) & (NZ - 1)
        packed = jnp.zeros((deep, LANES), F32)
        for g in range(NZ):
            part = total[g * deep : (g + 1) * deep]
            part = pltpu.roll(part, ((g - to_z) * own) & (LANES - 1), 1)
            packed = jnp.where(place == g, part, packed)
        out_ref[chunk:, :] = jnp.concatenate([packed, jnp.zeros_like(packed)], axis=0).astype(BF16)


def score_chunk(place, dense, pieces, sums):
    steps = 2
    chunk = dense.shape[0] // 2
    width = dense.shape[1]
    share = pieces[0].shape[1]
    extra = sums is not None
    out_rows = chunk + (2 * sums[0].shape[0] // NZ if extra else 0)
    more = tuple(sums) if extra else ()
    halves = dense.reshape(2, chunk, width)
    vmem = pl.BlockSpec(memory_space=pltpu.VMEM)
    return pl.pallas_call(
        functools.partial(score_kernel, extra=extra),
        out_shape=[jax.ShapeDtypeStruct((out_rows, LANES), BF16)] * NZ,
        grid_spec=pltpu.PrefetchScalarGridSpec(
            num_scalar_prefetch=1,
            grid=(steps,),
            in_specs=[pl.BlockSpec((2, chunk // steps, width), lambda i, s: (0, i, 0))]
            + [vmem] * (len(pieces) + len(more)),
            out_specs=[vmem] * NZ,
            scratch_shapes=[pltpu.VMEM((NZ, chunk, LANES), BF16)],
        ),
        compiler_params=pltpu.CompilerParams(vmem_limit_bytes=20 << 20),
        cost_estimate=pl.CostEstimate(
            flops=2 * chunk * width * share * 2, transcendentals=0, bytes_accessed=chunk * width * 4
        ),
        name="score_chunk",
    )(place, kept_in_hbm(halves), *pieces, *more)


def cut_kernel(pos_ref, impact_ref, query_ref, named_ref, *refs, shifts):
    rows_ref, out_refs, named_here, sem = refs[0], refs[1:-2], refs[-2], refs[-1]
    x, core = pos_ref[0], pos_ref[2]
    full, width = query_ref.shape
    count = len(out_refs) * CUTS
    copies = [
        pltpu.make_async_copy(named_ref, named_here, sem.at[count]),
        pltpu.make_async_copy(query_ref, rows_ref.at[:, pl.ds(0, width)], sem.at[count + 1]),
    ]
    for i, (out_ref, r) in enumerate(zip(out_refs, shifts)):
        depth, share = out_ref.shape
        part = depth // CUTS
        to_x = (x - r) & (NX - 1)
        for j in range(CUTS):
            at = (pl.ds(core * depth + j * part, part), pl.ds(to_x * share, share))
            copies.append(
                pltpu.make_async_copy(impact_ref.at[at], out_ref.at[pl.ds(j * part, part)], sem.at[i * CUTS + j])
            )
    for copy in copies:
        copy.start()
    copies[0].wait()
    named = named_here[...].astype(F32)
    named = jnp.concatenate([named, jnp.zeros((LANES - CANDS, full), F32)], axis=0)
    rows_ref[:, width:] = named.T.astype(BF16)
    for copy in copies[1:]:
        copy.wait()


def cut_slices(place, impact, query_rows, candidates, shifts):
    full, width = query_rows.shape
    one = jax.ShapeDtypeStruct((impact.shape[0] // 2, impact.shape[1] // NX), BF16)
    vmem = pl.BlockSpec(memory_space=pltpu.VMEM)
    hbm = pl.BlockSpec(memory_space=pltpu.HBM)
    rows, *cuts = pl.pallas_call(
        functools.partial(cut_kernel, shifts=shifts),
        out_shape=[jax.ShapeDtypeStruct((full, width + LANES), BF16)] + [one] * len(shifts),
        in_specs=[pl.BlockSpec(memory_space=pltpu.SMEM), hbm, hbm, hbm],
        out_specs=[vmem] * (1 + len(shifts)),
        scratch_shapes=[
            pltpu.VMEM((CANDS, full), jnp.int32),
            pltpu.SemaphoreType.DMA((len(shifts) * CUTS + 2,)),
        ],
        compiler_params=pltpu.CompilerParams(vmem_limit_bytes=4 << 20),
        name="cut_slices",
    )(place, kept_in_hbm(impact), kept_in_hbm(query_rows), kept_in_hbm(candidates.T))
    return rows, cuts


def final_kernel(pos_ref, a0, a1, a2, b0, b1, b2, v0, v1, v2, v3, first_ref, rescored_ref):
    x = pos_ref[0]
    half = LANES // 2
    chunk = b0.shape[0]
    column = 0
    for own, one, two in ((a0, a1, a2), (b0, b1, b2)):
        total = own[:chunk].astype(F32) + one[:chunk].astype(F32) + two[:chunk].astype(F32)
        turned = total.T.astype(BF16)
        first_ref[:, column : column + chunk] = turned[:half]
        first_ref[:, column + chunk : column + 2 * chunk] = turned[half:]
        column += 2 * chunk
    more = v0[...].astype(F32) + v1[...].astype(F32) + v2[...].astype(F32) + v3[...].astype(F32)
    share = LANES // (NX * NZ)
    deep = more.shape[0] // 2
    turned = pltpu.roll(more, (LANES - x * (LANES // NX)) & (LANES - 1), 1).T
    for g in range(NZ):
        part = turned[g * share : (g + 1) * share, :deep]
        rescored_ref[g // 2, :, (g % 2) * deep : (g % 2 + 1) * deep] = part


def finish(place, parts, sums, full):
    chunk = parts[3].shape[0]
    vmem = pl.BlockSpec(memory_space=pltpu.VMEM)
    return pl.pallas_call(
        final_kernel,
        out_shape=[
            jax.ShapeDtypeStruct((LANES // 2, 4 * chunk), BF16),
            jax.ShapeDtypeStruct((CANDS, LANES // (NX * NZ), full), F32),
        ],
        in_specs=[pl.BlockSpec(memory_space=pltpu.SMEM)] + [vmem] * 10,
        out_specs=[vmem] * 2,
        compiler_params=pltpu.CompilerParams(vmem_limit_bytes=8 << 20),
        name="finish",
    )(place, *parts, *sums)


def added(*parts):
    total = parts[0].astype(F32)
    for part in parts[1:]:
        total = total + part.astype(F32)
    return total.astype(BF16)


def after(values, done):
    return lax.optimization_barrier((values, done))[0]


def sent(values):
    out = {}
    for way in (1, -1):
        out[way] = shifted(values[way], "z", way)
    return out


def first_step(made, long_way):
    ahead = shifted(made[4], "z", 2 * long_way)
    return ahead, sent({1: made[3], -1: made[5]})


def second_values(made, long_way, ahead, carried):
    values = {1: [carried[1], made[2]], -1: [carried[-1], made[6]]}
    values[long_way].append(ahead)
    return {way: added(*parts) for way, parts in values.items()}


def third_values(made, carried):
    return {1: added(carried[1], made[1]), -1: added(carried[-1], made[7])}


def rings(made_a, made_b, start_a, start_b):
    (ahead_a, going_a), (ahead_b, going_b) = start_a, start_b
    going_a = sent(second_values(made_a, 1, ahead_a, going_a))
    going_b = sent(second_values(made_b, -1, ahead_b, going_b))
    going_a = sent(third_values(made_a, going_a))
    going_b = sent(third_values(made_b, going_b))
    return (going_a[1], going_a[-1]), (going_b[1], going_b[-1])


def scored(term_ids, term_weights, impact, query_rows, candidates):
    x = lax.axis_index("x")
    z = lax.axis_index("z")
    y = lax.axis_index("prange")
    core = lax.axis_index("query")
    place = jnp.stack([x, z, core, y]).astype(jnp.int32)
    shard_width, passages = impact.shape
    full = query_rows.shape[0]
    half_terms = shard_width // 2
    share = passages // NX

    def cut(whole, half, to_x):
        return lax.dynamic_slice(whole, (half * half_terms, to_x * share), (half_terms, share))

    shifts = (1, 3, 2)
    rows, cuts = cut_slices(place, impact, query_rows, candidates, shifts)
    near = {r: shifted(one, "x", -r) for r, one in zip(shifts, cuts)}
    (term_ids, term_weights), rows = lax.optimization_barrier(((term_ids, term_weights), rows))
    gathered = [rows] + [shifted(rows, "prange", -r) for r in (1, 2, 3)]

    ids = term_ids.T
    weights = term_weights.T
    dense_a = build_dense(place, ids, weights, NX * shard_width, 0)
    gathered = after(gathered, dense_a)
    by_home = score_rows(place, gathered, impact)
    back = [by_home[0]] + [shifted(by_home[r], "prange", r) for r in (1, 2, 3)]
    ids = after(ids, by_home)
    dense_b = build_dense(place, ids, weights, NX * shard_width, 1)

    impact, near, back = after((impact, near, back), dense_b)
    pieces = [cut(impact, core, x), cut(impact, 1 - core, x)]
    for r in (1, 2, 3):
        pieces += [near[r], shifted(near[r], "query", 1)]
    made_a = score_chunk(place, dense_a, pieces, back)
    start_a = first_step(made_a, 1)
    made_b = score_chunk(place, dense_b, pieces, None)
    start_b = first_step(made_b, -1)
    (a1, a2), (b1, b2) = rings(made_a, made_b, start_a, start_b)
    chunk = made_b[0].shape[0]
    mine = added(made_a[0][chunk:], a1[chunk:], a2[chunk:])
    sums = [mine]
    for r in (1, 2, 3):
        sums.append(shifted(mine, "x", r))
    first, rescored = finish(place, (made_a[0], a1, a2, made_b[0], b1, b2), sums, full)
    return (first[None], jnp.transpose(rescored, (2, 0, 1)))


def solution(mesh):
    finer = Mesh(
        mesh.devices.reshape(NX, NZ, mesh.shape["prange"], mesh.shape["query"]),
        ("x", "z", "prange", "query"),
    )
    vocab = ("x", "z")
    in_specs = (
        P("query", None),
        P("query", None),
        P(vocab, "prange"),
        P(("prange", "query"), vocab),
        P(("prange", "query"), None),
    )
    out_specs = (P("prange", vocab, "query"), P(("prange", "query"), None, vocab))
    return jax.shard_map(scored, mesh=finer, in_specs=in_specs, out_specs=out_specs, check_vma=False)
```

profile of v0, /device:TPU:2, one launch (start us, length us, event | category | flops | bytes accessed | tf_op | source)
XLA Modules:
  0.0 110.1 jit_solution(15431394875916246758)
XLA Ops:
  0.6 0.1 pad_add_fusion.pos_ref
  0.7 2.1 %cut_slices.1 = (bf16[16,1152]{1,0:T(8,128)(2,1)S(1)}, bf16[512,512]{1,0:T(8,128)(2,1)S(1)}, bf16[512,512]{1,0:T(8,128)(2,1)S(1)}, bf16[512,512]{1,0:T(8,128)(2,1)S(1)}) custom-call(s32[4]{0:T(128)S(1)} %pad_add_fusion.pos_ref, bf16[1024,2048]{1,0:T(8,128)(2,1)} %impact_ref.3, bf16[16,1024]{1,0:T(8,128)(2,1)} %query_ref.1, s32[4,16]{1,0:T(4,128)} %bitcast.11), custom_call_target="tpu_custom_call" | custom-call | tf_op jit(solution)/shard_map/cut_slices/pallas_call | solution.py:256
  2.9 1.7 %collective-permute-start.5 = (bf16[16,1152]{1,0:T(8,128)(2,1)S(1)}, bf16[16,1152]{1,0:T(8,128)(2,1)S(1)}, u32[]{:S(2)}, u32[]{:S(2)}) collective-permute-start(bf16[16,1152]{1,0:T(8,128)(2,1)S(1)} %get-tuple-element.51.r0), channel_id=1, source_target_pairs={{0,2},{2,4},{4,6},{6,0},{1,3},{3,5},{5,7},{7,1},{8,10},{10,12},{12... | collective-permute-start | bytes 110600 | tf_op jit(solution)/shard_map/ppermute | solution.py:29
  4.5 2.9 %collective-permute-start.4 = (bf16[16,1152]{1,0:T(8,128)(2,1)S(1)}, bf16[16,1152]{1,0:T(8,128)(2,1)S(1)}, u32[]{:S(2)}, u32[]{:S(2)}) collective-permute-start(bf16[16,1152]{1,0:T(8,128)(2,1)S(1)} %get-tuple-element.51.r0), channel_id=1, source_target_pairs={{0,4},{2,6},{4,0},{6,2},{1,5},{3,7},{5,1},{7,3},{8,12},{10,14},{12... | collective-permute-start | bytes 110600 | tf_op jit(solution)/shard_map/ppermute | solution.py:29
  7.4 1.3 %collective-permute-start.3 = (bf16[16,1152]{1,0:T(8,128)(2,1)S(1)}, bf16[16,1152]{1,0:T(8,128)(2,1)S(1)}, u32[]{:S(2)}, u32[]{:S(2)}) collective-permute-start(bf16[16,1152]{1,0:T(8,128)(2,1)S(1)} %get-tuple-element.51.r0), channel_id=1, source_target_pairs={{0,6},{2,0},{4,2},{6,4},{1,7},{3,1},{5,3},{7,5},{8,14},{10,8},{12,... | collective-permute-start | bytes 110600 | tf_op jit(solution)/shard_map/ppermute | solution.py:29
  8.8 9.8 %dense_build.2 = bf16[1024,4096]{1,0:T(8,128)(2,1)} custom-call(s32[4]{0:T(128)S(1)} %pad_add_fusion.pos_ref, s32[32,2048]{1,0:T(8,128)} %bitcast.12, bf16[32,2048]{1,0:T(8,128)(2,1)} %bitcast.15), custom_call_target="tpu_custom_call" | custom-call | flops 10000000000 | bytes 8388608 | tf_op jit(solution)/shard_map/dense_build/pallas_call | solution.py:92
  18.6 0.0 collective-permute-done.5.r3
  18.6 0.0 collective-permute-done.4.r2
  18.6 0.0 collective-permute-done.3.r1
  18.6 1.5 %score_rows.1 = (bf16[64,128]{1,0:T(8,128)(2,1)S(1)}, bf16[64,128]{1,0:T(8,128)(2,1)S(1)}, bf16[64,128]{1,0:T(8,128)(2,1)S(1)}, bf16[64,128]{1,0:T(8,128)(2,1)S(1)}) custom-call(s32[4]{0:T(128)S(1)} %pad_add_fusion.pos_ref, bf16[16,1152]{1,0:T(8,128)(2,1)S(1)} %get-tuple-element.51.r0, bf16[16,1152]{1,0:T(8,128)(2,1)S(1)} %collective-permute-done.3.r1, ...), custom_call_target="tpu_custom_call" | custom-call | flops 2000000000 | bytes 4194304 | tf_op jit(solution)/shard_map/score_rows/pallas_call | solution.py:130
  20.1 0.7 collective-permute-start.6
  20.8 0.6 collective-permute-start
  21.4 2.4 %collective-permute-start.1 = (bf16[512,512]{1,0:T(8,128)(2,1)S(1)}, bf16[512,512]{1,0:T(8,128)(2,1)S(1)}, u32[]{:S(2)}, u32[]{:S(2)}) collective-permute-start(bf16[512,512]{1,0:T(8,128)(2,1)S(1)} %get-tuple-element.48), channel_id=1, source_target_pairs={{0,128},{64,192},{128,0},{192,64},{1,129},{65,193},{129,1},{193,65... | collective-permute-start | bytes 1572872 | tf_op jit(solution)/shard_map/ppermute | solution.py:29
  23.8 1.8 %collective-permute-start.2 = (bf16[512,512]{1,0:T(8,128)(2,1)S(1)}, bf16[512,512]{1,0:T(8,128)(2,1)S(1)}, u32[]{:S(2)}, u32[]{:S(2)}) collective-permute-start(bf16[512,512]{1,0:T(8,128)(2,1)S(1)} %get-tuple-element.49), channel_id=1, source_target_pairs={{0,64},{64,128},{128,192},{192,0},{1,65},{65,129},{129,193},{193,1... | collective-permute-start | bytes 1572872 | tf_op jit(solution)/shard_map/ppermute | solution.py:29
  25.6 0.8 collective-permute-start.7
  26.4 0.0 collective-permute-done.6.refs_9_
  26.4 2.0 %collective-permute-start.8 = (bf16[64,128]{1,0:T(8,128)(2,1)S(1)}, bf16[64,128]{1,0:T(8,128)(2,1)S(1)}, u32[]{:S(2)}, u32[]{:S(2)}) collective-permute-start(bf16[64,128]{1,0:T(8,128)(2,1)S(1)} %get-tuple-element.58), channel_id=1, source_target_pairs={{0,6},{2,0},{4,2},{6,4},{1,7},{3,1},{5,3},{7,5},{8,14},{10,8},{12,... | collective-permute-start | bytes 49160 | tf_op jit(solution)/shard_map/ppermute | solution.py:29
  28.4 9.4 %dense_build.3 = bf16[1024,4096]{1,0:T(8,128)(2,1)} custom-call(s32[4]{0:T(128)S(1)} %pad_add_fusion.pos_ref, s32[32,2048]{1,0:T(8,128)} %bitcast.13, bf16[32,2048]{1,0:T(8,128)(2,1)} %bitcast.16), custom_call_target="tpu_custom_call" | custom-call | flops 10000000000 | bytes 8388608 | tf_op jit(solution)/shard_map/dense_build/pallas_call | solution.py:92
  37.8 0.0 collective-permute-done.7.refs_10_
  37.8 0.0 collective-permute-done.8.refs_11_
  37.8 0.0 collective-permute-done.refs_2_
  37.8 7.7 %collective-permute-done.1.refs_4_ = bf16[512,512]{1,0:T(8,128)(2,1)S(1)} collective-permute-done((bf16[512,512]{1,0:T(8,128)(2,1)S(1)}, bf16[512,512]{1,0:T(8,128)(2,1)S(1)}, u32[]{:S(2)}, u32[]{:S(2)}) %collective-permute-start.1) | collective-permute-done | bytes 524320 | tf_op jit(solution)/shard_map/ppermute | solution.py:29
  45.6 0.9 collective-permute-done.2.refs_6_
  46.5 0.0 collective-permute-start.9
  46.5 0.5 collective-permute-start.10
  47.0 0.0 collective-permute-start.11
  47.0 1.3 %fusion = (bf16[512,512]{1,0:T(8,128)(2,1)S(1)}, bf16[512,512]{1,0:T(8,128)(2,1)S(1)}) fusion(bf16[1024,2048]{1,0:T(8,128)(2,1)} %impact_ref.3, s32[]{:T(128)S(6)} %select_n.12, s32[]{:T(128)S(6)} %select_n.11, s32[]{:T(128)S(6)} %select_n.10), kind=kLoop, calls=%fused_computation.10 | loop fusion | bytes 2097164 | tf_op jit(solution)/shard_map/dynamic_slice | solution.py:361
  48.2 0.1 collective-permute-done.9.refs_3_
  48.4 0.7 collective-permute-done.10.refs_5_
  49.1 0.7 collective-permute-done.11.refs_7_
  49.9 7.8 %score_chunk.3 = (bf16[512,128]{1,0:T(8,128)(2,1)S(1)}, bf16[512,128]{1,0:T(8,128)(2,1)S(1)}, bf16[512,128]{1,0:T(8,128)(2,1)S(1)}, bf16[512,128]{1,0:T(8,128)(2...) custom-call(s32[4]{0:T(128)S(1)} %pad_add_fusion.pos_ref, ...), custom_call_target="tpu_custom_call" | custom-call | flops 4294967296 | bytes 8388608 | tf_op jit(solution)/shard_map/score_chunk/pallas_call | solution.py:204
  57.7 2.0 %collective-permute-start.19 = (bf16[512,128]{1,0:T(8,128)(2,1)S(1)}, bf16[512,128]{1,0:T(8,128)(2,1)S(1)}, u32[]{:S(2)}, u32[]{:S(2)}) collective-permute-start(bf16[512,128]{1,0:T(8,128)(2,1)S(1)} %get-tuple-element.77), channel_id=1, source_target_pairs={{0,8},{8,16},{16,24},{24,32},{32,40},{40,48},{48,56},{56,0},{1,9},... | collective-permute-start | bytes 393224 | tf_op jit(solution)/shard_map/ppermute | solution.py:29
  59.7 4.0 %collective-permute-start.22 = (bf16[512,128]{1,0:T(8,128)(2,1)S(1)}, bf16[512,128]{1,0:T(8,128)(2,1)S(1)}, u32[]{:S(2)}, u32[]{:S(2)}) collective-permute-start(bf16[512,128]{1,0:T(8,128)(2,1)S(1)} %get-tuple-element.80), channel_id=1, source_target_pairs={{0,56},{8,0},{16,8},{24,16},{32,24},{40,32},{48,40},{56,48},{1,57}... | collective-permute-start | bytes 393224 | tf_op jit(solution)/shard_map/ppermute | solution.py:29
  63.7 2.4 %collective-permute-start.23 = (bf16[512,128]{1,0:T(8,128)(2,1)S(1)}, bf16[512,128]{1,0:T(8,128)(2,1)S(1)}, u32[]{:S(2)}, u32[]{:S(2)}) collective-permute-start(bf16[512,128]{1,0:T(8,128)(2,1)S(1)} %get-tuple-element.82), channel_id=1, source_target_pairs={{0,48},{8,56},{16,0},{24,8},{32,16},{40,24},{48,32},{56,40},{1,49}... | collective-permute-start | bytes 393224 | tf_op jit(solution)/shard_map/ppermute | solution.py:29
  66.1 7.9 %score_chunk.2 = (bf16[528,128]{1,0:T(8,128)(2,1)S(1)}, bf16[528,128]{1,0:T(8,128)(2,1)S(1)}, bf16[528,128]{1,0:T(8,128)(2,1)S(1)}, bf16[528,128]{1,0:T(8,128)(2...) custom-call(s32[4]{0:T(128)S(1)} %pad_add_fusion.pos_ref, ...), custom_call_target="tpu_custom_call" | custom-call | flops 4294967296 | bytes 8388608 | tf_op jit(solution)/shard_map/score_chunk/pallas_call | solution.py:204
  74.0 1.1 collective-permute-start.12
  75.1 0.0 collective-permute-start.13
  75.1 0.0 collective-permute-done.19
  75.1 2.8 %collective-permute-start.16 = (bf16[528,128]{1,0:T(8,128)(2,1)S(1)}, bf16[528,128]{1,0:T(8,128)(2,1)S(1)}, u32[]{:S(2)}, u32[]{:S(2)}) collective-permute-start(bf16[528,128]{1,0:T(8,128)(2,1)S(1)} %get-tuple-element.73), channel_id=1, source_target_pairs={{0,56},{8,0},{16,8},{24,16},{32,24},{40,32},{48,40},{56,48},{1,57}... | collective-permute-start | bytes 405512 | tf_op jit(solution)/shard_map/ppermute | solution.py:29
  78.0 0.1 collective-permute-start.20
  78.1 0.1 add_convert_fusion.5
  78.1 3.3 %collective-permute-start.24 = (bf16[512,128]{1,0:T(8,128)(2,1)S(1)}, bf16[512,128]{1,0:T(8,128)(2,1)S(1)}, u32[]{:S(2)}, u32[]{:S(2)}) collective-permute-start(bf16[512,128]{1,0:T(8,128)(2,1)S(1)} %add_convert_fusion.5), channel_id=1, source_target_pairs={{0,56},{8,0},{16,8},{24,16},{32,24},{40,32},{48,40},{56,48},{1,57}... | collective-permute-start | bytes 393224 | tf_op jit(solution)/shard_map/ppermute | solution.py:29
  81.4 3.0 %collective-permute-done.12 = bf16[528,128]{1,0:T(8,128)(2,1)S(1)} collective-permute-done((bf16[528,128]{1,0:T(8,128)(2,1)S(1)}, bf16[528,128]{1,0:T(8,128)(2,1)S(1)}, u32[]{:S(2)}, u32[]{:S(2)}) %collective-permute-start.12) | collective-permute-done | bytes 135200 | tf_op jit(solution)/shard_map/ppermute | solution.py:29
  84.4 1.0 collective-permute-done.13
  85.4 0.1 add_convert_fusion.3
  85.5 3.7 %collective-permute-start.14 = (bf16[528,128]{1,0:T(8,128)(2,1)S(1)}, bf16[528,128]{1,0:T(8,128)(2,1)S(1)}, u32[]{:S(2)}, u32[]{:S(2)}) collective-permute-start(bf16[528,128]{1,0:T(8,128)(2,1)S(1)} %add_convert_fusion.3), channel_id=1, source_target_pairs={{0,8},{8,16},{16,24},{24,32},{32,40},{40,48},{48,56},{56,0},{1,9},... | collective-permute-start | bytes 405512 | tf_op jit(solution)/shard_map/ppermute | solution.py:29
  89.2 0.0 collective-permute-done.16
  89.2 0.1 collective-permute-start.17
  89.3 0.9 collective-permute-done.20
  90.2 1.4 %collective-permute-start.21 = (bf16[512,128]{1,0:T(8,128)(2,1)S(1)}, bf16[512,128]{1,0:T(8,128)(2,1)S(1)}, u32[]{:S(2)}, u32[]{:S(2)}) collective-permute-start(bf16[512,128]{1,0:T(8,128)(2,1)S(1)} %add_convert_fusion.6), channel_id=1, source_target_pairs={{0,8},{8,16},{16,24},{24,32},{32,40},{40,48},{48,56},{56,0},{1,9},... | collective-permute-start | bytes 393224 | tf_op jit(solution)/shard_map/ppermute | solution.py:29
  91.7 1.1 %collective-permute-done.14 = bf16[528,128]{1,0:T(8,128)(2,1)S(1)} collective-permute-done((bf16[528,128]{1,0:T(8,128)(2,1)S(1)}, bf16[528,128]{1,0:T(8,128)(2,1)S(1)}, u32[]{:S(2)}, u32[]{:S(2)}) %collective-permute-start.14) | collective-permute-done | bytes 135200 | tf_op jit(solution)/shard_map/ppermute | solution.py:29
  92.8 2.6 %collective-permute-start.15 = (bf16[528,128]{1,0:T(8,128)(2,1)S(1)}, bf16[528,128]{1,0:T(8,128)(2,1)S(1)}, u32[]{:S(2)}, u32[]{:S(2)}) collective-permute-start(bf16[528,128]{1,0:T(8,128)(2,1)S(1)} %add_convert_fusion.2), channel_id=1, source_target_pairs={{0,8},{8,16},{16,24},{24,32},{32,40},{40,48},{48,56},{56,0},{1,9},... | collective-permute-start | bytes 405512 | tf_op jit(solution)/shard_map/ppermute | solution.py:29
  95.4 0.3 collective-permute-done.17
  95.7 0.6 collective-permute-start.18
  96.3 0.8 collective-permute-start.25
  97.2 2.0 %collective-permute-done.15.a1 = bf16[528,128]{1,0:T(8,128)(2,1)S(1)} collective-permute-done((bf16[528,128]{1,0:T(8,128)(2,1)S(1)}, bf16[528,128]{1,0:T(8,128)(2,1)S(1)}, u32[]{:S(2)}, u32[]{:S(2)}) %collective-permute-start.15) | collective-permute-done | bytes 135200 | tf_op jit(solution)/shard_map/ppermute | solution.py:29
  99.1 1.7 %collective-permute-done.18.a2 = bf16[528,128]{1,0:T(8,128)(2,1)S(1)} collective-permute-done((bf16[528,128]{1,0:T(8,128)(2,1)S(1)}, bf16[528,128]{1,0:T(8,128)(2,1)S(1)}, u32[]{:S(2)}, u32[]{:S(2)}) %collective-permute-start.18) | collective-permute-done | bytes 135200 | tf_op jit(solution)/shard_map/ppermute | solution.py:29
  100.8 2.7 %collective-permute-start.28 = (bf16[16,128]{1,0:T(8,128)(2,1)S(1)}, bf16[16,128]{1,0:T(8,128)(2,1)S(1)}, u32[]{:S(2)}, u32[]{:S(2)}) collective-permute-start(bf16[16,128]{1,0:T(8,128)(2,1)S(1)} %add_convert_fusion.8.v0), channel_id=1, source_target_pairs={{0,192},{64,0},{128,64},{192,128},{1,193},{65,1},{129,65},{193,129... | collective-permute-start | bytes 12296 | tf_op jit(solution)/shard_map/ppermute | solution.py:29
  103.5 0.2 collective-permute-start.27
  103.7 1.9 %collective-permute-start.26 = (bf16[16,128]{1,0:T(8,128)(2,1)S(1)}, bf16[16,128]{1,0:T(8,128)(2,1)S(1)}, u32[]{:S(2)}, u32[]{:S(2)}) collective-permute-start(bf16[16,128]{1,0:T(8,128)(2,1)S(1)} %add_convert_fusion.8.v0), channel_id=1, source_target_pairs={{0,64},{64,128},{128,192},{192,0},{1,65},{65,129},{129,193},{193,1... | collective-permute-start | bytes 12296 | tf_op jit(solution)/shard_map/ppermute | solution.py:29
  105.6 0.0 collective-permute-done.21.b1
  105.6 3.0 %collective-permute-done.27.v2 = bf16[16,128]{1,0:T(8,128)(2,1)S(1)} collective-permute-done((bf16[16,128]{1,0:T(8,128)(2,1)S(1)}, bf16[16,128]{1,0:T(8,128)(2,1)S(1)}, u32[]{:S(2)}, u32[]{:S(2)}) %collective-permute-start.27) | collective-permute-done | bytes 4128 | tf_op jit(solution)/shard_map/ppermute | solution.py:29
  108.6 0.0 collective-permute-done.26.v1
  108.6 1.4 %finish.1 = (bf16[64,2048]{1,0:T(8,128)(2,1)}, f32[4,4,16]{2,1,0:T(4,128)}) custom-call(s32[4]{0:T(128)S(1)} %pad_add_fusion.pos_ref, bf16[528,128]{1,0:T(8,128)(2,1)S(1)} %get-tuple-element.68.a0, bf16[528,128]{1,0:T(8,128)(2,1)S(1)} %collective-permute-done.15.a1, bf16[528,128]{1,0:T(8,128)(2,1)S(1)} %collective-permute-done.18.a2, ...), custom_call_target="tpu_custom_call" | custom-call | tf_op jit(solution)/shard_map/finish/pallas_call | solution.py:294
  (14 shorter events, 0.3 us)
Async XLA Ops:
  2.9 15.7 %collective-permute-start.5 = (bf16[16,1152]{1,0:T(8,128)(2,1)S(1)}, bf16[16,1152]{1,0:T(8,128)(2,1)S(1)}, u32[]{:S(2)}, u32[]{:S(2)}) collective-permute-start(bf16[16,1152]{1,0:T(8,128)(2,1)S(1)} %get-tuple-element.51.r0), channel_id=1, source_target_pairs={{0,2},{2,4},{4,6},{6,0},{1,3},{3,5},{5,7},{7,1},{8,10},{10,12},{12... | collective-permute-start | bytes 110600 | tf_op jit(solution)/shard_map/ppermute | solution.py:29
  4.5 14.1 %collective-permute-start.4 = (bf16[16,1152]{1,0:T(8,128)(2,1)S(1)}, bf16[16,1152]{1,0:T(8,128)(2,1)S(1)}, u32[]{:S(2)}, u32[]{:S(2)}) collective-permute-start(bf16[16,1152]{1,0:T(8,128)(2,1)S(1)} %get-tuple-element.51.r0), channel_id=1, source_target_pairs={{0,4},{2,6},{4,0},{6,2},{1,5},{3,7},{5,1},{7,3},{8,12},{10,14},{12... | collective-permute-start | bytes 110600 | tf_op jit(solution)/shard_map/ppermute | solution.py:29
  7.4 11.2 %collective-permute-start.3 = (bf16[16,1152]{1,0:T(8,128)(2,1)S(1)}, bf16[16,1152]{1,0:T(8,128)(2,1)S(1)}, u32[]{:S(2)}, u32[]{:S(2)}) collective-permute-start(bf16[16,1152]{1,0:T(8,128)(2,1)S(1)} %get-tuple-element.51.r0), channel_id=1, source_target_pairs={{0,6},{2,0},{4,2},{6,4},{1,7},{3,1},{5,3},{7,5},{8,14},{10,8},{12,... | collective-permute-start | bytes 110600 | tf_op jit(solution)/shard_map/ppermute | solution.py:29
  8.8 9.8 %copy-start = (bf16[1024,2048]{1,0:T(8,128)(2,1)S(1)}, bf16[1024,2048]{1,0:T(8,128)(2,1)}, u32[]{:S(2)}) copy-start(bf16[1024,2048]{1,0:T(8,128)(2,1)} %impact_ref.3) | copy-start | bytes 12582916
  20.1 6.3 %collective-permute-start.6 = (bf16[64,128]{1,0:T(8,128)(2,1)S(1)}, bf16[64,128]{1,0:T(8,128)(2,1)S(1)}, u32[]{:S(2)}, u32[]{:S(2)}) collective-permute-start(bf16[64,128]{1,0:T(8,128)(2,1)S(1)} %get-tuple-element.56), channel_id=1, source_target_pairs={{0,2},{2,4},{4,6},{6,0},{1,3},{3,5},{5,7},{7,1},{8,10},{10,12},{12... | collective-permute-start | bytes 49160 | tf_op jit(solution)/shard_map/ppermute | solution.py:29
  20.8 17.0 %collective-permute-start = (bf16[512,512]{1,0:T(8,128)(2,1)S(1)}, bf16[512,512]{1,0:T(8,128)(2,1)S(1)}, u32[]{:S(2)}, u32[]{:S(2)}) collective-permute-start(bf16[512,512]{1,0:T(8,128)(2,1)S(1)} %get-tuple-element.47), channel_id=1, source_target_pairs={{0,192},{64,0},{128,64},{192,128},{1,193},{65,1},{129,65},{193,129... | collective-permute-start | bytes 1572872 | tf_op jit(solution)/shard_map/ppermute | solution.py:29
  21.4 24.2 %collective-permute-start.1 = (bf16[512,512]{1,0:T(8,128)(2,1)S(1)}, bf16[512,512]{1,0:T(8,128)(2,1)S(1)}, u32[]{:S(2)}, u32[]{:S(2)}) collective-permute-start(bf16[512,512]{1,0:T(8,128)(2,1)S(1)} %get-tuple-element.48), channel_id=1, source_target_pairs={{0,128},{64,192},{128,0},{192,64},{1,129},{65,193},{129,1},{193,65... | collective-permute-start | bytes 1572872 | tf_op jit(solution)/shard_map/ppermute | solution.py:29
  23.8 22.7 %collective-permute-start.2 = (bf16[512,512]{1,0:T(8,128)(2,1)S(1)}, bf16[512,512]{1,0:T(8,128)(2,1)S(1)}, u32[]{:S(2)}, u32[]{:S(2)}) collective-permute-start(bf16[512,512]{1,0:T(8,128)(2,1)S(1)} %get-tuple-element.49), channel_id=1, source_target_pairs={{0,64},{64,128},{128,192},{192,0},{1,65},{65,129},{129,193},{193,1... | collective-permute-start | bytes 1572872 | tf_op jit(solution)/shard_map/ppermute | solution.py:29
  25.6 12.2 %collective-permute-start.7 = (bf16[64,128]{1,0:T(8,128)(2,1)S(1)}, bf16[64,128]{1,0:T(8,128)(2,1)S(1)}, u32[]{:S(2)}, u32[]{:S(2)}) collective-permute-start(bf16[64,128]{1,0:T(8,128)(2,1)S(1)} %get-tuple-element.57), channel_id=1, source_target_pairs={{0,4},{2,6},{4,0},{6,2},{1,5},{3,7},{5,1},{7,3},{8,12},{10,14},{12... | collective-permute-start | bytes 49160 | tf_op jit(solution)/shard_map/ppermute | solution.py:29
  26.4 11.4 %collective-permute-start.8 = (bf16[64,128]{1,0:T(8,128)(2,1)S(1)}, bf16[64,128]{1,0:T(8,128)(2,1)S(1)}, u32[]{:S(2)}, u32[]{:S(2)}) collective-permute-start(bf16[64,128]{1,0:T(8,128)(2,1)S(1)} %get-tuple-element.58), channel_id=1, source_target_pairs={{0,6},{2,0},{4,2},{6,4},{1,7},{3,1},{5,3},{7,5},{8,14},{10,8},{12,... | collective-permute-start | bytes 49160 | tf_op jit(solution)/shard_map/ppermute | solution.py:29
  46.5 1.9 %collective-permute-start.9 = (bf16[512,512]{1,0:T(8,128)(2,1)S(1)}, bf16[512,512]{1,0:T(8,128)(2,1)S(1)}, u32[]{:S(2)}, u32[]{:S(2)}) collective-permute-start(bf16[512,512]{1,0:T(8,128)(2,1)S(1)} %collective-permute-done.refs_2_), channel_id=1, source_target_pairs={{0,1},{1,0},{2,3},{3,2},{4,5},{5,4},{6,7},{7,6},{8,9},{9,8},{10,11... | collective-permute-start | bytes 1572872 | tf_op jit(solution)/shard_map/ppermute | solution.py:29
  46.5 2.7 %collective-permute-start.10 = (bf16[512,512]{1,0:T(8,128)(2,1)S(1)}, bf16[512,512]{1,0:T(8,128)(2,1)S(1)}, u32[]{:S(2)}, u32[]{:S(2)}) collective-permute-start(bf16[512,512]{1,0:T(8,128)(2,1)S(1)} %collective-permute-done.1.refs_4_), channel_id=1, source_target_pairs={{0,1},{1,0},{2,3},{3,2},{4,5},{5,4},{6,7},{7,6},{8,9},{9,8},{10,11... | collective-permute-start | bytes 1572872 | tf_op jit(solution)/shard_map/ppermute | solution.py:29
  47.0 2.9 %collective-permute-start.11 = (bf16[512,512]{1,0:T(8,128)(2,1)S(1)}, bf16[512,512]{1,0:T(8,128)(2,1)S(1)}, u32[]{:S(2)}, u32[]{:S(2)}) collective-permute-start(bf16[512,512]{1,0:T(8,128)(2,1)S(1)} %collective-permute-done.2.refs_6_), channel_id=1, source_target_pairs={{0,1},{1,0},{2,3},{3,2},{4,5},{5,4},{6,7},{7,6},{8,9},{9,8},{10,11... | collective-permute-start | bytes 1572872 | tf_op jit(solution)/shard_map/ppermute | solution.py:29
  57.7 17.4 %collective-permute-start.19 = (bf16[512,128]{1,0:T(8,128)(2,1)S(1)}, bf16[512,128]{1,0:T(8,128)(2,1)S(1)}, u32[]{:S(2)}, u32[]{:S(2)}) collective-permute-start(bf16[512,128]{1,0:T(8,128)(2,1)S(1)} %get-tuple-element.77), channel_id=1, source_target_pairs={{0,8},{8,16},{16,24},{24,32},{32,40},{40,48},{48,56},{56,0},{1,9},... | collective-permute-start | bytes 393224 | tf_op jit(solution)/shard_map/ppermute | solution.py:29
  59.7 18.2 %collective-permute-start.22 = (bf16[512,128]{1,0:T(8,128)(2,1)S(1)}, bf16[512,128]{1,0:T(8,128)(2,1)S(1)}, u32[]{:S(2)}, u32[]{:S(2)}) collective-permute-start(bf16[512,128]{1,0:T(8,128)(2,1)S(1)} %get-tuple-element.80), channel_id=1, source_target_pairs={{0,56},{8,0},{16,8},{24,16},{32,24},{40,32},{48,40},{56,48},{1,57}... | collective-permute-start | bytes 393224 | tf_op jit(solution)/shard_map/ppermute | solution.py:29
  63.7 14.3 %collective-permute-start.23 = (bf16[512,128]{1,0:T(8,128)(2,1)S(1)}, bf16[512,128]{1,0:T(8,128)(2,1)S(1)}, u32[]{:S(2)}, u32[]{:S(2)}) collective-permute-start(bf16[512,128]{1,0:T(8,128)(2,1)S(1)} %get-tuple-element.82), channel_id=1, source_target_pairs={{0,48},{8,56},{16,0},{24,8},{32,16},{40,24},{48,32},{56,40},{1,49}... | collective-permute-start | bytes 393224 | tf_op jit(solution)/shard_map/ppermute | solution.py:29
  74.0 10.3 %collective-permute-start.12 = (bf16[528,128]{1,0:T(8,128)(2,1)S(1)}, bf16[528,128]{1,0:T(8,128)(2,1)S(1)}, u32[]{:S(2)}, u32[]{:S(2)}) collective-permute-start(bf16[528,128]{1,0:T(8,128)(2,1)S(1)} %get-tuple-element.69), channel_id=1, source_target_pairs={{0,8},{8,16},{16,24},{24,32},{32,40},{40,48},{48,56},{56,0},{1,9},... | collective-permute-start | bytes 405512 | tf_op jit(solution)/shard_map/ppermute | solution.py:29
  75.1 10.3 %collective-permute-start.13 = (bf16[528,128]{1,0:T(8,128)(2,1)S(1)}, bf16[528,128]{1,0:T(8,128)(2,1)S(1)}, u32[]{:S(2)}, u32[]{:S(2)}) collective-permute-start(bf16[528,128]{1,0:T(8,128)(2,1)S(1)} %get-tuple-element.71), channel_id=1, source_target_pairs={{0,16},{8,24},{16,32},{24,40},{32,48},{40,56},{48,0},{56,8},{1,17}... | collective-permute-start | bytes 405512 | tf_op jit(solution)/shard_map/ppermute | solution.py:29
  75.1 14.0 %collective-permute-start.16 = (bf16[528,128]{1,0:T(8,128)(2,1)S(1)}, bf16[528,128]{1,0:T(8,128)(2,1)S(1)}, u32[]{:S(2)}, u32[]{:S(2)}) collective-permute-start(bf16[528,128]{1,0:T(8,128)(2,1)S(1)} %get-tuple-element.73), channel_id=1, source_target_pairs={{0,56},{8,0},{16,8},{24,16},{32,24},{40,32},{48,40},{56,48},{1,57}... | collective-permute-start | bytes 405512 | tf_op jit(solution)/shard_map/ppermute | solution.py:29
  78.0 12.2 %collective-permute-start.20 = (bf16[512,128]{1,0:T(8,128)(2,1)S(1)}, bf16[512,128]{1,0:T(8,128)(2,1)S(1)}, u32[]{:S(2)}, u32[]{:S(2)}) collective-permute-start(bf16[512,128]{1,0:T(8,128)(2,1)S(1)} %add_convert_fusion.7), channel_id=1, source_target_pairs={{0,8},{8,16},{16,24},{24,32},{32,40},{40,48},{48,56},{56,0},{1,9},... | collective-permute-start | bytes 393224 | tf_op jit(solution)/shard_map/ppermute | solution.py:29
  78.1 18.2 %collective-permute-start.24 = (bf16[512,128]{1,0:T(8,128)(2,1)S(1)}, bf16[512,128]{1,0:T(8,128)(2,1)S(1)}, u32[]{:S(2)}, u32[]{:S(2)}) collective-permute-start(bf16[512,128]{1,0:T(8,128)(2,1)S(1)} %add_convert_fusion.5), channel_id=1, source_target_pairs={{0,56},{8,0},{16,8},{24,16},{32,24},{40,32},{48,40},{56,48},{1,57}... | collective-permute-start | bytes 393224 | tf_op jit(solution)/shard_map/ppermute | solution.py:29
  85.5 7.3 %collective-permute-start.14 = (bf16[528,128]{1,0:T(8,128)(2,1)S(1)}, bf16[528,128]{1,0:T(8,128)(2,1)S(1)}, u32[]{:S(2)}, u32[]{:S(2)}) collective-permute-start(bf16[528,128]{1,0:T(8,128)(2,1)S(1)} %add_convert_fusion.3), channel_id=1, source_target_pairs={{0,8},{8,16},{16,24},{24,32},{32,40},{40,48},{48,56},{56,0},{1,9},... | collective-permute-start | bytes 405512 | tf_op jit(solution)/shard_map/ppermute | solution.py:29
  89.2 6.4 %collective-permute-start.17 = (bf16[528,128]{1,0:T(8,128)(2,1)S(1)}, bf16[528,128]{1,0:T(8,128)(2,1)S(1)}, u32[]{:S(2)}, u32[]{:S(2)}) collective-permute-start(bf16[528,128]{1,0:T(8,128)(2,1)S(1)} %add_convert_fusion.1), channel_id=1, source_target_pairs={{0,56},{8,0},{16,8},{24,16},{32,24},{40,32},{48,40},{56,48},{1,57}... | collective-permute-start | bytes 405512 | tf_op jit(solution)/shard_map/ppermute | solution.py:29
  90.2 15.4 %collective-permute-start.21 = (bf16[512,128]{1,0:T(8,128)(2,1)S(1)}, bf16[512,128]{1,0:T(8,128)(2,1)S(1)}, u32[]{:S(2)}, u32[]{:S(2)}) collective-permute-start(bf16[512,128]{1,0:T(8,128)(2,1)S(1)} %add_convert_fusion.6), channel_id=1, source_target_pairs={{0,8},{8,16},{16,24},{24,32},{32,40},{40,48},{48,56},{56,0},{1,9},... | collective-permute-start | bytes 393224 | tf_op jit(solution)/shard_map/ppermute | solution.py:29
  92.8 6.3 %collective-permute-start.15 = (bf16[528,128]{1,0:T(8,128)(2,1)S(1)}, bf16[528,128]{1,0:T(8,128)(2,1)S(1)}, u32[]{:S(2)}, u32[]{:S(2)}) collective-permute-start(bf16[528,128]{1,0:T(8,128)(2,1)S(1)} %add_convert_fusion.2), channel_id=1, source_target_pairs={{0,8},{8,16},{16,24},{24,32},{32,40},{40,48},{48,56},{56,0},{1,9},... | collective-permute-start | bytes 405512 | tf_op jit(solution)/shard_map/ppermute | solution.py:29
  95.7 5.1 %collective-permute-start.18 = (bf16[528,128]{1,0:T(8,128)(2,1)S(1)}, bf16[528,128]{1,0:T(8,128)(2,1)S(1)}, u32[]{:S(2)}, u32[]{:S(2)}) collective-permute-start(bf16[528,128]{1,0:T(8,128)(2,1)S(1)} %add_convert_fusion), channel_id=1, source_target_pairs={{0,56},{8,0},{16,8},{24,16},{32,24},{40,32},{48,40},{56,48},{1,57}... | collective-permute-start | bytes 405512 | tf_op jit(solution)/shard_map/ppermute | solution.py:29
  96.3 9.3 %collective-permute-start.25 = (bf16[512,128]{1,0:T(8,128)(2,1)S(1)}, bf16[512,128]{1,0:T(8,128)(2,1)S(1)}, u32[]{:S(2)}, u32[]{:S(2)}) collective-permute-start(bf16[512,128]{1,0:T(8,128)(2,1)S(1)} %add_convert_fusion.4), channel_id=1, source_target_pairs={{0,56},{8,0},{16,8},{24,16},{32,24},{40,32},{48,40},{56,48},{1,57}... | collective-permute-start | bytes 393224 | tf_op jit(solution)/shard_map/ppermute | solution.py:29
  100.8 4.8 %collective-permute-start.28 = (bf16[16,128]{1,0:T(8,128)(2,1)S(1)}, bf16[16,128]{1,0:T(8,128)(2,1)S(1)}, u32[]{:S(2)}, u32[]{:S(2)}) collective-permute-start(bf16[16,128]{1,0:T(8,128)(2,1)S(1)} %add_convert_fusion.8.v0), channel_id=1, source_target_pairs={{0,192},{64,0},{128,64},{192,128},{1,193},{65,1},{129,65},{193,129... | collective-permute-start | bytes 12296 | tf_op jit(solution)/shard_map/ppermute | solution.py:29
  103.5 5.1 %collective-permute-start.27 = (bf16[16,128]{1,0:T(8,128)(2,1)S(1)}, bf16[16,128]{1,0:T(8,128)(2,1)S(1)}, u32[]{:S(2)}, u32[]{:S(2)}) collective-permute-start(bf16[16,128]{1,0:T(8,128)(2,1)S(1)} %add_convert_fusion.8.v0), channel_id=1, source_target_pairs={{0,128},{64,192},{128,0},{192,64},{1,129},{65,193},{129,1},{193,65... | collective-permute-start | bytes 12296 | tf_op jit(solution)/shard_map/ppermute | solution.py:29
  103.7 4.9 %collective-permute-start.26 = (bf16[16,128]{1,0:T(8,128)(2,1)S(1)}, bf16[16,128]{1,0:T(8,128)(2,1)S(1)}, u32[]{:S(2)}, u32[]{:S(2)}) collective-permute-start(bf16[16,128]{1,0:T(8,128)(2,1)S(1)} %add_convert_fusion.8.v0), channel_id=1, source_target_pairs={{0,64},{64,128},{128,192},{192,0},{1,65},{65,129},{129,193},{193,1... | collective-permute-start | bytes 12296 | tf_op jit(solution)/shard_map/ppermute | solution.py:29
where the time goes:
time: 110 us
  starting transfers between devices  44.3 us (40%)
  Pallas kernels  40.1 us (36%)
  waiting for transfers between devices  23.2 us (21%)
  local copies, waits for them, and re-layouts  1.28 us (1%)
    ppermute x29, starting transfers between devices, shifted(): lax.ppermute(array, axis, [(i, (i + shift) % size) for i in range(size)])  44.3 us
    ppermute x29, waiting for transfers between devices, shifted(): lax.ppermute(array, axis, [(i, (i + shift) % size) for i in range(size)])  23.2 us
    pallas_call x2, Pallas kernels, build_dense(): pl.pallas_call(dense_kernel, out_shape=pltpu.HBM((queries * blocks, width...  19.3 us
    pallas_call x2, Pallas kernels, score_chunk(): pl.pallas_call(functools.partial(score_kernel, extra=extra), out_shape=[j...  15.8 us
  transfers between devices with their start and end apart: 29, of which 13 were waited for; matrix products, arithmetic and copies ran while one was open for 1% of the time, Pallas kernels for 25%

commit v1 on v0

--- a/solution.py
+++ b/solution.py
@@ -82,27 +82,21 @@
     lax.fori_loop(0, groups // 2, pair_of_groups, 0, unroll=UNROLL)
 
 
-def build_dense(place, ids, weights, width, chunk):
-    blocks = 2
-    terms = ids.shape[0]
-    queries = ids.shape[1] // CHUNKS // blocks
+def build_dense(place, ids, weights, width):
+    terms, queries = ids.shape
     groups = queries // GROUP
-    spec = pl.BlockSpec((terms, queries), lambda i, s: (0, chunk * blocks + i))
     rows = pltpu.VMEM((groups, GROUP * terms), F32)
+    vmem = pl.BlockSpec(memory_space=pltpu.VMEM)
     return pl.pallas_call(
         dense_kernel,
-        out_shape=pltpu.HBM((queries * blocks, width), BF16),
-        grid_spec=pltpu.PrefetchScalarGridSpec(
-            num_scalar_prefetch=1,
-            grid=(blocks,),
-            in_specs=[spec, spec],
-            out_specs=pl.BlockSpec((queries, width), lambda i, s: (i, 0)),
-            scratch_shapes=[pltpu.VMEM((queries, LANES), F32), rows, rows, rows],
-        ),
-        compiler_params=pltpu.CompilerParams(vmem_limit_bytes=12 << 20),
-        cost_estimate=pl.CostEstimate(flops=10**10, transcendentals=0, bytes_accessed=queries * blocks * width * 2),
+        out_shape=pltpu.VMEM((queries, width), BF16),
+        in_specs=[pl.BlockSpec(memory_space=pltpu.SMEM), vmem, vmem],
+        out_specs=vmem,
+        scratch_shapes=[pltpu.VMEM((queries, LANES), F32), rows, rows, rows],
+        compiler_params=pltpu.CompilerParams(vmem_limit_bytes=6 << 20),
+        cost_estimate=pl.CostEstimate(flops=10**10, transcendentals=0, bytes_accessed=queries * width * 2),
         name="dense_build",
-    )(place, kept_in_hbm(ids), kept_in_hbm(weights))
+    )(place, ids, weights)
 
 
 def rows_kernel(pos_ref, r0, r1, r2, r3, impact_ref, o0, o1, o2, o3):
@@ -138,40 +132,44 @@
     )(place, *gathered, impact)
 
 
-def score_kernel(pos_ref, dense_ref, *refs, extra):
-    piece_refs = refs[:8]
-    extra_refs = refs[8:12] if extra else ()
-    out_refs = refs[-NZ - 1 : -1]
-    made_ref = refs[-1]
-    z = pos_ref[1]
-    rows, _ = dense_ref.shape[1:]
-    depth = piece_refs[0].shape[0]
+def score_kernel(pos_ref, impact_ref, dense_ref, *refs, extra, steps):
+    piece_refs = refs[:6]
+    extra_refs = refs[6:10] if extra else ()
+    out_refs = refs[-NZ - 3 : -3]
+    made_ref, own_ref, own_sem = refs[-3:]
+    x, z, core = pos_ref[0], pos_ref[1], pos_ref[2]
+    depth, share = piece_refs[0].shape
     chunk = made_ref.shape[1]
+    rows = chunk // steps
     half = LANES // 2
-    step = pl.program_id(0)
-    last = step == pl.num_programs(0) - 1
-    made = []
-    for part in range(2):
-        total = None
-        for i, piece in enumerate(piece_refs):
-            block = dense_ref[part, :, i * depth : (i + 1) * depth]
-            one = jnp.dot(block, piece[...], preferred_element_type=F32)
-            total = one if total is None else total + one
-        made.append(total)
+    copies = []
+    for i in range(2):
+        at = (pl.ds((core ^ i) * depth, depth), pl.ds(x * share, share))
+        copies.append(pltpu.make_async_copy(impact_ref.at[at], own_ref.at[i], own_sem.at[i]))
+        copies[i].start()
     left = lax.broadcasted_iota(jnp.int32, (rows, LANES), 1) < half
-    at = pl.ds(pl.multiple_of(step * rows, rows), rows)
-    for m in range(NZ // 2):
-        a = made[0][:, m * LANES : (m + 1) * LANES]
-        b = made[1][:, m * LANES : (m + 1) * LANES]
-        made_ref[2 * m, at, :] = jnp.where(left, a, pltpu.roll(b, half, 1)).astype(BF16)
-        made_ref[2 * m + 1, at, :] = jnp.where(left, pltpu.roll(a, half, 1), b).astype(BF16)
-
-    @pl.when(last)
-    def _():
-        for j, out_ref in enumerate(out_refs):
-            out_ref[:chunk, :] = made_ref[(z + j) & (NZ - 1)]
-        if extra:
-            pack_rows(z, chunk, extra_refs, out_refs)
+    for step in range(steps):
+        made = [None, None]
+        for i in (2, 3, 4, 5, 6, 7, 0, 1):
+            if step == 0 and i == 0:
+                for copy in copies:
+                    copy.wait()
+            piece = own_ref[i] if i < 2 else piece_refs[i - 2][...]
+            for part in range(2):
+                first = part * chunk + step * rows
+                block = dense_ref[first : first + rows, i * depth : (i + 1) * depth]
+                one = jnp.dot(block, piece, preferred_element_type=F32)
+                made[part] = one if made[part] is None else made[part] + one
+        for m in range(NZ // 2):
+            a = made[0][:, m * LANES : (m + 1) * LANES]
+            b = made[1][:, m * LANES : (m + 1) * LANES]
+            at = slice(step * rows, (step + 1) * rows)
+            made_ref[2 * m, at, :] = jnp.where(left, a, pltpu.roll(b, half, 1)).astype(BF16)
+            made_ref[2 * m + 1, at, :] = jnp.where(left, pltpu.roll(a, half, 1), b).astype(BF16)
+    for j, out_ref in enumerate(out_refs):
+        out_ref[:chunk, :] = made_ref[(z + j) & (NZ - 1)]
+    if extra:
+        pack_rows(z, chunk, extra_refs, out_refs)
 
 
 def pack_rows(z, chunk, extra_refs, out_refs):
@@ -191,33 +189,31 @@
         out_ref[chunk:, :] = jnp.concatenate([packed, jnp.zeros_like(packed)], axis=0).astype(BF16)
 
 
-def score_chunk(place, dense, pieces, sums):
-    steps = 2
+def score_chunk(place, impact, dense, pieces, sums):
     chunk = dense.shape[0] // 2
     width = dense.shape[1]
-    share = pieces[0].shape[1]
+    depth, share = pieces[0].shape
     extra = sums is not None
     out_rows = chunk + (2 * sums[0].shape[0] // NZ if extra else 0)
     more = tuple(sums) if extra else ()
-    halves = dense.reshape(2, chunk, width)
     vmem = pl.BlockSpec(memory_space=pltpu.VMEM)
+    hbm = pl.BlockSpec(memory_space=pltpu.HBM)
     return pl.pallas_call(
-        functools.partial(score_kernel, extra=extra),
+        functools.partial(score_kernel, extra=extra, steps=2),
         out_shape=[jax.ShapeDtypeStruct((out_rows, LANES), BF16)] * NZ,
-        grid_spec=pltpu.PrefetchScalarGridSpec(
-            num_scalar_prefetch=1,
-            grid=(steps,),
-            in_specs=[pl.BlockSpec((2, chunk // steps, width), lambda i, s: (0, i, 0))]
-            + [vmem] * (len(pieces) + len(more)),
-            out_specs=[vmem] * NZ,
-            scratch_shapes=[pltpu.VMEM((NZ, chunk, LANES), BF16)],
-        ),
-        compiler_params=pltpu.CompilerParams(vmem_limit_bytes=20 << 20),
+        in_specs=[pl.BlockSpec(memory_space=pltpu.SMEM), hbm] + [vmem] * (1 + len(pieces) + len(more)),
+        out_specs=[vmem] * NZ,
+        scratch_shapes=[
+            pltpu.VMEM((NZ, chunk, LANES), BF16),
+            pltpu.VMEM((2, depth, share), BF16),
+            pltpu.SemaphoreType.DMA((2,)),
+        ],
+        compiler_params=pltpu.CompilerParams(vmem_limit_bytes=12 << 20),
         cost_estimate=pl.CostEstimate(
             flops=2 * chunk * width * share * 2, transcendentals=0, bytes_accessed=chunk * width * 4
         ),
         name="score_chunk",
-    )(place, kept_in_hbm(halves), *pieces, *more)
+    )(place, kept_in_hbm(impact), dense, *pieces, *more)
 
 
 def cut_kernel(pos_ref, impact_ref, query_ref, named_ref, *refs, shifts):
@@ -352,13 +348,8 @@
     y = lax.axis_index("prange")
     core = lax.axis_index("query")
     place = jnp.stack([x, z, core, y]).astype(jnp.int32)
-    shard_width, passages = impact.shape
+    shard_width = impact.shape[0]
     full = query_rows.shape[0]
-    half_terms = shard_width // 2
-    share = passages // NX
-
-    def cut(whole, half, to_x):
-        return lax.dynamic_slice(whole, (half * half_terms, to_x * share), (half_terms, share))
 
     shifts = (1, 3, 2)
     rows, cuts = cut_slices(place, impact, query_rows, candidates, shifts)
@@ -368,20 +359,21 @@
 
     ids = term_ids.T
     weights = term_weights.T
-    dense_a = build_dense(place, ids, weights, NX * shard_width, 0)
+    half = ids.shape[1] // CHUNKS
+    dense_a = build_dense(place, ids[:, :half], weights[:, :half], NX * shard_width)
     gathered = after(gathered, dense_a)
     by_home = score_rows(place, gathered, impact)
     back = [by_home[0]] + [shifted(by_home[r], "prange", r) for r in (1, 2, 3)]
     ids = after(ids, by_home)
-    dense_b = build_dense(place, ids, weights, NX * shard_width, 1)
-
-    impact, near, back = after((impact, near, back), dense_b)
-    pieces = [cut(impact, core, x), cut(impact, 1 - core, x)]
+    dense_b = build_dense(place, ids[:, half:], weights[:, half:], NX * shard_width)
+
+    near, back = after((near, back), dense_b)
+    pieces = []
     for r in (1, 2, 3):
         pieces += [near[r], shifted(near[r], "query", 1)]
-    made_a = score_chunk(place, dense_a, pieces, back)
+    made_a = score_chunk(place, impact, dense_a, pieces, back)
     start_a = first_step(made_a, 1)
-    made_b = score_chunk(place, dense_b, pieces, None)
+    made_b = score_chunk(place, impact, dense_b, pieces, None)
     start_b = first_step(made_b, -1)
     (a1, a2), (b1, b2) = rings(made_a, made_b, start_a, start_b)
     chunk = made_b[0].shape[0]

time: 110 us -> 107 us (0.973)
  Pallas kernels: 40.1 us -> 31.9 us
  waiting for transfers between devices: 23.2 us -> 27.2 us
    pallas_call x4, Pallas kernels: 35 us -> 26.8 us  [the longest x2 13.9 us: build_dense(): pl.pallas_call(dense_kernel, out_shape=pltpu.VMEM((queries, width), BF16)...]
    ppermute x29, waiting for transfers between devices: 23.2 us -> 27.2 us  [shifted(): lax.ppermute(array, axis, [(i, (i + shift) % size) for i in range(size)])]
    slice x0 -> x3, local copies, waits for them, and re-layouts: none -> 1.81 us  [the longest x1 0.91 us: scored(): ids[:, :half]]
    dynamic_slice x1 -> x0, local copies, waits for them, and re-layouts: 1.27 us -> none  [cut(): lax.dynamic_slice(whole, (half * half_terms, to_x * share), (half_terms,...]
  transfers between devices with their start and end apart: 29 -> 29, of which waited for: 13 -> 13; matrix products, arithmetic and copies ran while one was open for 1% -> 2% of each run, Pallas kernels for 25% -> 19%
where the time goes in v1:
time: 107 us; the launch traced here: 106 us
  starting transfers between devices  44.1 us (41%)
  Pallas kernels  31.9 us (30%)
  waiting for transfers between devices  27.2 us (25%)
  local copies, waits for them, and re-layouts  1.82 us (2%)
    ppermute x29, starting transfers between devices, shifted(): lax.ppermute(array, axis, [(i, (i + shift) % size) for i in range(size)])  44.1 us
    ppermute x29, waiting for transfers between devices, shifted(): lax.ppermute(array, axis, [(i, (i + shift) % size) for i in range(size)])  27.2 us
    pallas_call x2, Pallas kernels, build_dense(): pl.pallas_call(dense_kernel, out_shape=pltpu.VMEM((queries, width), BF16)...  13.9 us
    pallas_call x2, Pallas kernels, score_chunk(): pl.pallas_call(functools.partial(score_kernel, extra=extra, steps=2), out...  13 us
    pallas_call x1, Pallas kernels, cut_slices(): pl.pallas_call(functools.partial(cut_kernel, shifts=shifts), out_shape=[j...  2.15 us
  transfers between devices with their start and end apart: 29, of which 13 were waited for; matrix products, arithmetic and copies ran while one was open for 2% of the time, Pallas kernels for 19%

profile of v1, /device:TPU:2, one launch (start us, length us, event | category | flops | bytes accessed | tf_op | source)
XLA Modules:
  0.0 106.2 jit_solution(11391992049780237262)
XLA Ops:
  0.6 0.1 pad_add_fusion.pos_ref
  0.7 2.1 %cut_slices.1 = (bf16[16,1152]{1,0:T(8,128)(2,1)S(1)}, bf16[512,512]{1,0:T(8,128)(2,1)S(1)}, bf16[512,512]{1,0:T(8,128)(2,1)S(1)}, bf16[512,512]{1,0:T(8,128)(2,1)S(1)}) custom-call(s32[4]{0:T(128)S(1)} %pad_add_fusion.pos_ref, bf16[1024,2048]{1,0:T(8,128)(2,1)} %impact_ref.7, bf16[16,1024]{1,0:T(8,128)(2,1)} %query_ref.1, s32[4,16]{1,0:T(4,128)} %bitcast.12), custom_call_target="tpu_custom_call" | custom-call | tf_op jit(solution)/shard_map/cut_slices/pallas_call | solution.py:252
  2.9 1.7 %collective-permute-start.5 = (bf16[16,1152]{1,0:T(8,128)(2,1)S(1)}, bf16[16,1152]{1,0:T(8,128)(2,1)S(1)}, u32[]{:S(2)}, u32[]{:S(2)}) collective-permute-start(bf16[16,1152]{1,0:T(8,128)(2,1)S(1)} %get-tuple-element.50.r0), channel_id=1, source_target_pairs={{0,2},{2,4},{4,6},{6,0},{1,3},{3,5},{5,7},{7,1},{8,10},{10,12},{12... | collective-permute-start | bytes 110600 | tf_op jit(solution)/shard_map/ppermute | solution.py:29
  4.5 2.9 %collective-permute-start.4 = (bf16[16,1152]{1,0:T(8,128)(2,1)S(1)}, bf16[16,1152]{1,0:T(8,128)(2,1)S(1)}, u32[]{:S(2)}, u32[]{:S(2)}) collective-permute-start(bf16[16,1152]{1,0:T(8,128)(2,1)S(1)} %get-tuple-element.50.r0), channel_id=1, source_target_pairs={{0,4},{2,6},{4,0},{6,2},{1,5},{3,7},{5,1},{7,3},{8,12},{10,14},{12... | collective-permute-start | bytes 110600 | tf_op jit(solution)/shard_map/ppermute | solution.py:29
  7.4 1.3 %collective-permute-start.3 = (bf16[16,1152]{1,0:T(8,128)(2,1)S(1)}, bf16[16,1152]{1,0:T(8,128)(2,1)S(1)}, u32[]{:S(2)}, u32[]{:S(2)}) collective-permute-start(bf16[16,1152]{1,0:T(8,128)(2,1)S(1)} %get-tuple-element.50.r0), channel_id=1, source_target_pairs={{0,6},{2,0},{4,2},{6,4},{1,7},{3,1},{5,3},{7,5},{8,14},{10,8},{12,... | collective-permute-start | bytes 110600 | tf_op jit(solution)/shard_map/ppermute | solution.py:29
  8.8 0.9 slice.28.ids_ref
  9.7 0.9 fusion
  10.6 0.0 copy-start
  10.6 0.0 copy-start.1
  10.6 6.9 %dense_build.2.dense_ref = bf16[1024,4096]{1,0:T(8,128)(2,1)S(1)} custom-call(s32[4]{0:T(128)S(1)} %pad_add_fusion.pos_ref, s32[32,1024]{1,0:T(8,128)S(1)} %slice.28.ids_ref, bf16[32,1024]{1,0:T(8,128)(2,1)S(1)} %get-tuple-element.85.weights_ref), custom_call_target="tpu_custom_call" | custom-call | flops 10000000000 | bytes 8388608 | tf_op jit(solution)/shard_map/dense_build/pallas_call | solution.py:90
  17.6 0.0 collective-permute-done.4.r2
  17.6 0.0 collective-permute-done.3.r1
  17.6 1.5 %score_rows.1 = (bf16[64,128]{1,0:T(8,128)(2,1)S(1)}, bf16[64,128]{1,0:T(8,128)(2,1)S(1)}, bf16[64,128]{1,0:T(8,128)(2,1)S(1)}, bf16[64,128]{1,0:T(8,128)(2,1)S(1)}) custom-call(s32[4]{0:T(128)S(1)} %pad_add_fusion.pos_ref, bf16[16,1152]{1,0:T(8,128)(2,1)S(1)} %get-tuple-element.50.r0, bf16[16,1152]{1,0:T(8,128)(2,1)S(1)} %collective-permute-done.3.r1, ...), custom_call_target="tpu_custom_call" | custom-call | flops 2000000000 | bytes 4194304 | tf_op jit(solution)/shard_map/score_rows/pallas_call | solution.py:124
  19.1 0.8 collective-permute-start.6
  19.8 0.5 collective-permute-start
  20.4 2.4 %collective-permute-start.1 = (bf16[512,512]{1,0:T(8,128)(2,1)S(1)}, bf16[512,512]{1,0:T(8,128)(2,1)S(1)}, u32[]{:S(2)}, u32[]{:S(2)}) collective-permute-start(bf16[512,512]{1,0:T(8,128)(2,1)S(1)} %get-tuple-element.47), channel_id=1, source_target_pairs={{0,128},{64,192},{128,0},{192,64},{1,129},{65,193},{129,1},{193,65... | collective-permute-start | bytes 1572872 | tf_op jit(solution)/shard_map/ppermute | solution.py:29
  22.8 1.8 %collective-permute-start.2 = (bf16[512,512]{1,0:T(8,128)(2,1)S(1)}, bf16[512,512]{1,0:T(8,128)(2,1)S(1)}, u32[]{:S(2)}, u32[]{:S(2)}) collective-permute-start(bf16[512,512]{1,0:T(8,128)(2,1)S(1)} %get-tuple-element.48), channel_id=1, source_target_pairs={{0,64},{64,128},{128,192},{192,0},{1,65},{65,129},{129,193},{193,1... | collective-permute-start | bytes 1572872 | tf_op jit(solution)/shard_map/ppermute | solution.py:29
  24.6 0.8 collective-permute-start.7
  25.4 0.0 collective-permute-done.6.refs_7_
  25.4 2.2 %collective-permute-start.8 = (bf16[64,128]{1,0:T(8,128)(2,1)S(1)}, bf16[64,128]{1,0:T(8,128)(2,1)S(1)}, u32[]{:S(2)}, u32[]{:S(2)}) collective-permute-start(bf16[64,128]{1,0:T(8,128)(2,1)S(1)} %get-tuple-element.57), channel_id=1, source_target_pairs={{0,6},{2,0},{4,2},{6,4},{1,7},{3,1},{5,3},{7,5},{8,14},{10,8},{12,... | collective-permute-start | bytes 49160 | tf_op jit(solution)/shard_map/ppermute | solution.py:29
  27.6 6.9 %dense_build.3.dense_ref = bf16[1024,4096]{1,0:T(8,128)(2,1)S(1)} custom-call(s32[4]{0:T(128)S(1)} %pad_add_fusion.pos_ref, s32[32,1024]{1,0:T(8,128)S(1)} %slice.23.ids_ref, bf16[32,1024]{1,0:T(8,128)(2,1)S(1)} %get-tuple-element.84.weights_ref), custom_call_target="tpu_custom_call" | custom-call | flops 10000000000 | bytes 8388608 | tf_op jit(solution)/shard_map/dense_build/pallas_call | solution.py:90
  34.6 0.0 collective-permute-done.7.refs_8_
  34.6 9.9 %collective-permute-done.1.refs_2_ = bf16[512,512]{1,0:T(8,128)(2,1)S(1)} collective-permute-done((bf16[512,512]{1,0:T(8,128)(2,1)S(1)}, bf16[512,512]{1,0:T(8,128)(2,1)S(1)}, u32[]{:S(2)}, u32[]{:S(2)}) %collective-permute-start.1) | collective-permute-done | bytes 524320 | tf_op jit(solution)/shard_map/ppermute | solution.py:29
  44.5 0.9 collective-permute-done.2.refs_4_
  45.4 0.5 collective-permute-start.10
  46.0 0.0 collective-permute-start.11
  46.0 1.4 %collective-permute-done.9.refs_1_ = bf16[512,512]{1,0:T(8,128)(2,1)S(1)} collective-permute-done((bf16[512,512]{1,0:T(8,128)(2,1)S(1)}, bf16[512,512]{1,0:T(8,128)(2,1)S(1)}, u32[]{:S(2)}, u32[]{:S(2)}) %collective-permute-start.9) | collective-permute-done | bytes 524320 | tf_op jit(solution)/shard_map/ppermute | solution.py:29
  47.4 0.7 collective-permute-done.10.refs_3_
  48.1 0.7 collective-permute-done.11.refs_5_
  48.9 6.5 %score_chunk.3 = (bf16[512,128]{1,0:T(8,128)(2,1)S(1)}, bf16[512,128]{1,0:T(8,128)(2,1)S(1)}, bf16[512,128]{1,0:T(8,128)(2,1)S(1)}, bf16[512,128]{1,0:T(8,128)(2...) custom-call(s32[4]{0:T(128)S(1)} %pad_add_fusion.pos_ref, ...), custom_call_target="tpu_custom_call" | custom-call | flops 4294967296 | bytes 8388608 | tf_op jit(solution)/shard_map/score_chunk/pallas_call | solution.py:201
  55.3 2.0 %collective-permute-start.19 = (bf16[512,128]{1,0:T(8,128)(2,1)S(1)}, bf16[512,128]{1,0:T(8,128)(2,1)S(1)}, u32[]{:S(2)}, u32[]{:S(2)}) collective-permute-start(bf16[512,128]{1,0:T(8,128)(2,1)S(1)} %get-tuple-element.75), channel_id=1, source_target_pairs={{0,8},{8,16},{16,24},{24,32},{32,40},{40,48},{48,56},{56,0},{1,9},... | collective-permute-start | bytes 393224 | tf_op jit(solution)/shard_map/ppermute | solution.py:29
  57.3 4.0 %collective-permute-start.22 = (bf16[512,128]{1,0:T(8,128)(2,1)S(1)}, bf16[512,128]{1,0:T(8,128)(2,1)S(1)}, u32[]{:S(2)}, u32[]{:S(2)}) collective-permute-start(bf16[512,128]{1,0:T(8,128)(2,1)S(1)} %get-tuple-element.78), channel_id=1, source_target_pairs={{0,56},{8,0},{16,8},{24,16},{32,24},{40,32},{48,40},{56,48},{1,57}... | collective-permute-start | bytes 393224 | tf_op jit(solution)/shard_map/ppermute | solution.py:29
  61.4 2.4 %collective-permute-start.23 = (bf16[512,128]{1,0:T(8,128)(2,1)S(1)}, bf16[512,128]{1,0:T(8,128)(2,1)S(1)}, u32[]{:S(2)}, u32[]{:S(2)}) collective-permute-start(bf16[512,128]{1,0:T(8,128)(2,1)S(1)} %get-tuple-element.80), channel_id=1, source_target_pairs={{0,48},{8,56},{16,0},{24,8},{32,16},{40,24},{48,32},{56,40},{1,49}... | collective-permute-start | bytes 393224 | tf_op jit(solution)/shard_map/ppermute | solution.py:29
  63.8 6.5 %score_chunk.2 = (bf16[528,128]{1,0:T(8,128)(2,1)S(1)}, bf16[528,128]{1,0:T(8,128)(2,1)S(1)}, bf16[528,128]{1,0:T(8,128)(2,1)S(1)}, bf16[528,128]{1,0:T(8,128)(2...) custom-call(s32[4]{0:T(128)S(1)} %pad_add_fusion.pos_ref, ...), custom_call_target="tpu_custom_call" | custom-call | flops 4294967296 | bytes 8388608 | tf_op jit(solution)/shard_map/score_chunk/pallas_call | solution.py:201
  70.2 1.1 %collective-permute-start.12 = (bf16[528,128]{1,0:T(8,128)(2,1)S(1)}, bf16[528,128]{1,0:T(8,128)(2,1)S(1)}, u32[]{:S(2)}, u32[]{:S(2)}) collective-permute-start(bf16[528,128]{1,0:T(8,128)(2,1)S(1)} %get-tuple-element.67), channel_id=1, source_target_pairs={{0,8},{8,16},{16,24},{24,32},{32,40},{40,48},{48,56},{56,0},{1,9},... | collective-permute-start | bytes 405512 | tf_op jit(solution)/shard_map/ppermute | solution.py:29
  71.3 0.0 collective-permute-start.13
  71.3 0.0 collective-permute-done.19
  71.3 2.8 %collective-permute-start.16 = (bf16[528,128]{1,0:T(8,128)(2,1)S(1)}, bf16[528,128]{1,0:T(8,128)(2,1)S(1)}, u32[]{:S(2)}, u32[]{:S(2)}) collective-permute-start(bf16[528,128]{1,0:T(8,128)(2,1)S(1)} %get-tuple-element.71), channel_id=1, source_target_pairs={{0,56},{8,0},{16,8},{24,16},{32,24},{40,32},{48,40},{56,48},{1,57}... | collective-permute-start | bytes 405512 | tf_op jit(solution)/shard_map/ppermute | solution.py:29
  74.1 0.1 collective-permute-start.20
  74.2 0.0 collective-permute-done.23
  74.3 0.1 add_convert_fusion.5
  74.3 3.3 %collective-permute-start.24 = (bf16[512,128]{1,0:T(8,128)(2,1)S(1)}, bf16[512,128]{1,0:T(8,128)(2,1)S(1)}, u32[]{:S(2)}, u32[]{:S(2)}) collective-permute-start(bf16[512,128]{1,0:T(8,128)(2,1)S(1)} %add_convert_fusion.5), channel_id=1, source_target_pairs={{0,56},{8,0},{16,8},{24,16},{32,24},{40,32},{48,40},{56,48},{1,57}... | collective-permute-start | bytes 393224 | tf_op jit(solution)/shard_map/ppermute | solution.py:29
  77.6 2.9 %collective-permute-done.12 = bf16[528,128]{1,0:T(8,128)(2,1)S(1)} collective-permute-done((bf16[528,128]{1,0:T(8,128)(2,1)S(1)}, bf16[528,128]{1,0:T(8,128)(2,1)S(1)}, u32[]{:S(2)}, u32[]{:S(2)}) %collective-permute-start.12) | collective-permute-done | bytes 135200 | tf_op jit(solution)/shard_map/ppermute | solution.py:29
  80.5 1.1 %collective-permute-done.13 = bf16[528,128]{1,0:T(8,128)(2,1)S(1)} collective-permute-done((bf16[528,128]{1,0:T(8,128)(2,1)S(1)}, bf16[528,128]{1,0:T(8,128)(2,1)S(1)}, u32[]{:S(2)}, u32[]{:S(2)}) %collective-permute-start.13) | collective-permute-done | bytes 135200 | tf_op jit(solution)/shard_map/ppermute | solution.py:29
  81.7 0.1 add_convert_fusion.3
  81.7 3.7 %collective-permute-start.14 = (bf16[528,128]{1,0:T(8,128)(2,1)S(1)}, bf16[528,128]{1,0:T(8,128)(2,1)S(1)}, u32[]{:S(2)}, u32[]{:S(2)}) collective-permute-start(bf16[528,128]{1,0:T(8,128)(2,1)S(1)} %add_convert_fusion.3), channel_id=1, source_target_pairs={{0,8},{8,16},{16,24},{24,32},{32,40},{40,48},{48,56},{56,0},{1,9},... | collective-permute-start | bytes 405512 | tf_op jit(solution)/shard_map/ppermute | solution.py:29
  85.4 0.1 collective-permute-start.17
  85.5 0.9 collective-permute-done.20
  86.4 1.2 %collective-permute-start.21 = (bf16[512,128]{1,0:T(8,128)(2,1)S(1)}, bf16[512,128]{1,0:T(8,128)(2,1)S(1)}, u32[]{:S(2)}, u32[]{:S(2)}) collective-permute-start(bf16[512,128]{1,0:T(8,128)(2,1)S(1)} %add_convert_fusion.6), channel_id=1, source_target_pairs={{0,8},{8,16},{16,24},{24,32},{32,40},{40,48},{48,56},{56,0},{1,9},... | collective-permute-start | bytes 393224 | tf_op jit(solution)/shard_map/ppermute | solution.py:29
  87.6 1.8 %collective-permute-done.14 = bf16[528,128]{1,0:T(8,128)(2,1)S(1)} collective-permute-done((bf16[528,128]{1,0:T(8,128)(2,1)S(1)}, bf16[528,128]{1,0:T(8,128)(2,1)S(1)}, u32[]{:S(2)}, u32[]{:S(2)}) %collective-permute-start.14) | collective-permute-done | bytes 135200 | tf_op jit(solution)/shard_map/ppermute | solution.py:29
  89.4 2.1 %collective-permute-start.15 = (bf16[528,128]{1,0:T(8,128)(2,1)S(1)}, bf16[528,128]{1,0:T(8,128)(2,1)S(1)}, u32[]{:S(2)}, u32[]{:S(2)}) collective-permute-start(bf16[528,128]{1,0:T(8,128)(2,1)S(1)} %add_convert_fusion.2), channel_id=1, source_target_pairs={{0,8},{8,16},{16,24},{24,32},{32,40},{40,48},{48,56},{56,0},{1,9},... | collective-permute-start | bytes 405512 | tf_op jit(solution)/shard_map/ppermute | solution.py:29
  91.6 0.3 collective-permute-done.17
  91.9 1.0 collective-permute-start.18
  92.9 0.6 collective-permute-start.25
  93.5 2.2 %collective-permute-done.15.a1 = bf16[528,128]{1,0:T(8,128)(2,1)S(1)} collective-permute-done((bf16[528,128]{1,0:T(8,128)(2,1)S(1)}, bf16[528,128]{1,0:T(8,128)(2,1)S(1)}, u32[]{:S(2)}, u32[]{:S(2)}) %collective-permute-start.15) | collective-permute-done | bytes 135200 | tf_op jit(solution)/shard_map/ppermute | solution.py:29
  95.7 1.2 %collective-permute-done.18.a2 = bf16[528,128]{1,0:T(8,128)(2,1)S(1)} collective-permute-done((bf16[528,128]{1,0:T(8,128)(2,1)S(1)}, bf16[528,128]{1,0:T(8,128)(2,1)S(1)}, u32[]{:S(2)}, u32[]{:S(2)}) %collective-permute-start.18) | collective-permute-done | bytes 135200 | tf_op jit(solution)/shard_map/ppermute | solution.py:29
  97.0 2.7 %collective-permute-start.28 = (bf16[16,128]{1,0:T(8,128)(2,1)S(1)}, bf16[16,128]{1,0:T(8,128)(2,1)S(1)}, u32[]{:S(2)}, u32[]{:S(2)}) collective-permute-start(bf16[16,128]{1,0:T(8,128)(2,1)S(1)} %add_convert_fusion.8.v0), channel_id=1, source_target_pairs={{0,192},{64,0},{128,64},{192,128},{1,193},{65,1},{129,65},{193,129... | collective-permute-start | bytes 12296 | tf_op jit(solution)/shard_map/ppermute | solution.py:29
  99.7 0.2 collective-permute-start.27
  99.9 1.9 %collective-permute-start.26 = (bf16[16,128]{1,0:T(8,128)(2,1)S(1)}, bf16[16,128]{1,0:T(8,128)(2,1)S(1)}, u32[]{:S(2)}, u32[]{:S(2)}) collective-permute-start(bf16[16,128]{1,0:T(8,128)(2,1)S(1)} %add_convert_fusion.8.v0), channel_id=1, source_target_pairs={{0,64},{64,128},{128,192},{192,0},{1,65},{65,129},{129,193},{193,1... | collective-permute-start | bytes 12296 | tf_op jit(solution)/shard_map/ppermute | solution.py:29
  101.8 0.0 collective-permute-done.21.b1
  101.8 0.0 collective-permute-done.25.b2
  101.8 3.0 %collective-permute-done.27.v2 = bf16[16,128]{1,0:T(8,128)(2,1)S(1)} collective-permute-done((bf16[16,128]{1,0:T(8,128)(2,1)S(1)}, bf16[16,128]{1,0:T(8,128)(2,1)S(1)}, u32[]{:S(2)}, u32[]{:S(2)}) %collective-permute-start.27) | collective-permute-done | bytes 4128 | tf_op jit(solution)/shard_map/ppermute | solution.py:29
  104.8 0.0 collective-permute-done.26.v1
  104.8 1.4 %finish.1 = (bf16[64,2048]{1,0:T(8,128)(2,1)}, f32[4,4,16]{2,1,0:T(4,128)}) custom-call(s32[4]{0:T(128)S(1)} %pad_add_fusion.pos_ref, bf16[528,128]{1,0:T(8,128)(2,1)S(1)} %get-tuple-element.66.a0, bf16[528,128]{1,0:T(8,128)(2,1)S(1)} %collective-permute-done.15.a1, bf16[528,128]{1,0:T(8,128)(2,1)S(1)} %collective-permute-done.18.a2, ...), custom_call_target="tpu_custom_call" | custom-call | tf_op jit(solution)/shard_map/finish/pallas_call | solution.py:290
  (18 shorter events, 0.3 us)
Async XLA Ops:
  2.9 14.7 %collective-permute-start.5 = (bf16[16,1152]{1,0:T(8,128)(2,1)S(1)}, bf16[16,1152]{1,0:T(8,128)(2,1)S(1)}, u32[]{:S(2)}, u32[]{:S(2)}) collective-permute-start(bf16[16,1152]{1,0:T(8,128)(2,1)S(1)} %get-tuple-element.50.r0), channel_id=1, source_target_pairs={{0,2},{2,4},{4,6},{6,0},{1,3},{3,5},{5,7},{7,1},{8,10},{10,12},{12... | collective-permute-start | bytes 110600 | tf_op jit(solution)/shard_map/ppermute | solution.py:29
  4.5 13.0 %collective-permute-start.4 = (bf16[16,1152]{1,0:T(8,128)(2,1)S(1)}, bf16[16,1152]{1,0:T(8,128)(2,1)S(1)}, u32[]{:S(2)}, u32[]{:S(2)}) collective-permute-start(bf16[16,1152]{1,0:T(8,128)(2,1)S(1)} %get-tuple-element.50.r0), channel_id=1, source_target_pairs={{0,4},{2,6},{4,0},{6,2},{1,5},{3,7},{5,1},{7,3},{8,12},{10,14},{12... | collective-permute-start | bytes 110600 | tf_op jit(solution)/shard_map/ppermute | solution.py:29
  7.4 10.1 %collective-permute-start.3 = (bf16[16,1152]{1,0:T(8,128)(2,1)S(1)}, bf16[16,1152]{1,0:T(8,128)(2,1)S(1)}, u32[]{:S(2)}, u32[]{:S(2)}) collective-permute-start(bf16[16,1152]{1,0:T(8,128)(2,1)S(1)} %get-tuple-element.50.r0), channel_id=1, source_target_pairs={{0,6},{2,0},{4,2},{6,4},{1,7},{3,1},{5,3},{7,5},{8,14},{10,8},{12,... | collective-permute-start | bytes 110600 | tf_op jit(solution)/shard_map/ppermute | solution.py:29
  10.6 7.0 %copy-start = (bf16[1024,2048]{1,0:T(8,128)(2,1)S(1)}, bf16[1024,2048]{1,0:T(8,128)(2,1)}, u32[]{:S(2)}) copy-start(bf16[1024,2048]{1,0:T(8,128)(2,1)} %impact_ref.7) | copy-start | bytes 12582916
  10.6 14.8 %copy-start.1 = (s32[2048,32]{0,1:T(8,128)S(1)}, s32[2048,32]{0,1:T(8,128)}, u32[]{:S(2)}) copy-start(s32[2048,32]{0,1:T(8,128)} %param.5) | copy-start | bytes 786436
  19.1 6.3 %collective-permute-start.6 = (bf16[64,128]{1,0:T(8,128)(2,1)S(1)}, bf16[64,128]{1,0:T(8,128)(2,1)S(1)}, u32[]{:S(2)}, u32[]{:S(2)}) collective-permute-start(bf16[64,128]{1,0:T(8,128)(2,1)S(1)} %get-tuple-element.55), channel_id=1, source_target_pairs={{0,2},{2,4},{4,6},{6,0},{1,3},{3,5},{5,7},{7,1},{8,10},{10,12},{12... | collective-permute-start | bytes 49160 | tf_op jit(solution)/shard_map/ppermute | solution.py:29
  19.8 14.8 %collective-permute-start = (bf16[512,512]{1,0:T(8,128)(2,1)S(1)}, bf16[512,512]{1,0:T(8,128)(2,1)S(1)}, u32[]{:S(2)}, u32[]{:S(2)}) collective-permute-start(bf16[512,512]{1,0:T(8,128)(2,1)S(1)} %get-tuple-element.46), channel_id=1, source_target_pairs={{0,192},{64,0},{128,64},{192,128},{1,193},{65,1},{129,65},{193,129... | collective-permute-start | bytes 1572872 | tf_op jit(solution)/shard_map/ppermute | solution.py:29
  20.4 24.2 %collective-permute-start.1 = (bf16[512,512]{1,0:T(8,128)(2,1)S(1)}, bf16[512,512]{1,0:T(8,128)(2,1)S(1)}, u32[]{:S(2)}, u32[]{:S(2)}) collective-permute-start(bf16[512,512]{1,0:T(8,128)(2,1)S(1)} %get-tuple-element.47), channel_id=1, source_target_pairs={{0,128},{64,192},{128,0},{192,64},{1,129},{65,193},{129,1},{193,65... | collective-permute-start | bytes 1572872 | tf_op jit(solution)/shard_map/ppermute | solution.py:29
  22.8 22.7 %collective-permute-start.2 = (bf16[512,512]{1,0:T(8,128)(2,1)S(1)}, bf16[512,512]{1,0:T(8,128)(2,1)S(1)}, u32[]{:S(2)}, u32[]{:S(2)}) collective-permute-start(bf16[512,512]{1,0:T(8,128)(2,1)S(1)} %get-tuple-element.48), channel_id=1, source_target_pairs={{0,64},{64,128},{128,192},{192,0},{1,65},{65,129},{129,193},{193,1... | collective-permute-start | bytes 1572872 | tf_op jit(solution)/shard_map/ppermute | solution.py:29
  24.6 10.0 %collective-permute-start.7 = (bf16[64,128]{1,0:T(8,128)(2,1)S(1)}, bf16[64,128]{1,0:T(8,128)(2,1)S(1)}, u32[]{:S(2)}, u32[]{:S(2)}) collective-permute-start(bf16[64,128]{1,0:T(8,128)(2,1)S(1)} %get-tuple-element.56), channel_id=1, source_target_pairs={{0,4},{2,6},{4,0},{6,2},{1,5},{3,7},{5,1},{7,3},{8,12},{10,14},{12... | collective-permute-start | bytes 49160 | tf_op jit(solution)/shard_map/ppermute | solution.py:29
  25.4 9.2 %collective-permute-start.8 = (bf16[64,128]{1,0:T(8,128)(2,1)S(1)}, bf16[64,128]{1,0:T(8,128)(2,1)S(1)}, u32[]{:S(2)}, u32[]{:S(2)}) collective-permute-start(bf16[64,128]{1,0:T(8,128)(2,1)S(1)} %get-tuple-element.57), channel_id=1, source_target_pairs={{0,6},{2,0},{4,2},{6,4},{1,7},{3,1},{5,3},{7,5},{8,14},{10,8},{12,... | collective-permute-start | bytes 49160 | tf_op jit(solution)/shard_map/ppermute | solution.py:29
  45.4 1.9 %collective-permute-start.9 = (bf16[512,512]{1,0:T(8,128)(2,1)S(1)}, bf16[512,512]{1,0:T(8,128)(2,1)S(1)}, u32[]{:S(2)}, u32[]{:S(2)}) collective-permute-start(bf16[512,512]{1,0:T(8,128)(2,1)S(1)} %collective-permute-done.refs_0_), channel_id=1, source_target_pairs={{0,1},{1,0},{2,3},{3,2},{4,5},{5,4},{6,7},{7,6},{8,9},{9,8},{10,11... | collective-permute-start | bytes 1572872 | tf_op jit(solution)/shard_map/ppermute | solution.py:29
  45.4 2.7 %collective-permute-start.10 = (bf16[512,512]{1,0:T(8,128)(2,1)S(1)}, bf16[512,512]{1,0:T(8,128)(2,1)S(1)}, u32[]{:S(2)}, u32[]{:S(2)}) collective-permute-start(bf16[512,512]{1,0:T(8,128)(2,1)S(1)} %collective-permute-done.1.refs_2_), channel_id=1, source_target_pairs={{0,1},{1,0},{2,3},{3,2},{4,5},{5,4},{6,7},{7,6},{8,9},{9,8},{10,11... | collective-permute-start | bytes 1572872 | tf_op jit(solution)/shard_map/ppermute | solution.py:29
  46.0 2.9 %collective-permute-start.11 = (bf16[512,512]{1,0:T(8,128)(2,1)S(1)}, bf16[512,512]{1,0:T(8,128)(2,1)S(1)}, u32[]{:S(2)}, u32[]{:S(2)}) collective-permute-start(bf16[512,512]{1,0:T(8,128)(2,1)S(1)} %collective-permute-done.2.refs_4_), channel_id=1, source_target_pairs={{0,1},{1,0},{2,3},{3,2},{4,5},{5,4},{6,7},{7,6},{8,9},{9,8},{10,11... | collective-permute-start | bytes 1572872 | tf_op jit(solution)/shard_map/ppermute | solution.py:29
  55.3 16.0 %collective-permute-start.19 = (bf16[512,128]{1,0:T(8,128)(2,1)S(1)}, bf16[512,128]{1,0:T(8,128)(2,1)S(1)}, u32[]{:S(2)}, u32[]{:S(2)}) collective-permute-start(bf16[512,128]{1,0:T(8,128)(2,1)S(1)} %get-tuple-element.75), channel_id=1, source_target_pairs={{0,8},{8,16},{16,24},{24,32},{32,40},{40,48},{48,56},{56,0},{1,9},... | collective-permute-start | bytes 393224 | tf_op jit(solution)/shard_map/ppermute | solution.py:29
  57.3 16.8 %collective-permute-start.22 = (bf16[512,128]{1,0:T(8,128)(2,1)S(1)}, bf16[512,128]{1,0:T(8,128)(2,1)S(1)}, u32[]{:S(2)}, u32[]{:S(2)}) collective-permute-start(bf16[512,128]{1,0:T(8,128)(2,1)S(1)} %get-tuple-element.78), channel_id=1, source_target_pairs={{0,56},{8,0},{16,8},{24,16},{32,24},{40,32},{48,40},{56,48},{1,57}... | collective-permute-start | bytes 393224 | tf_op jit(solution)/shard_map/ppermute | solution.py:29
  61.4 12.9 %collective-permute-start.23 = (bf16[512,128]{1,0:T(8,128)(2,1)S(1)}, bf16[512,128]{1,0:T(8,128)(2,1)S(1)}, u32[]{:S(2)}, u32[]{:S(2)}) collective-permute-start(bf16[512,128]{1,0:T(8,128)(2,1)S(1)} %get-tuple-element.80), channel_id=1, source_target_pairs={{0,48},{8,56},{16,0},{24,8},{32,16},{40,24},{48,32},{56,40},{1,49}... | collective-permute-start | bytes 393224 | tf_op jit(solution)/shard_map/ppermute | solution.py:29
  70.2 10.3 %collective-permute-start.12 = (bf16[528,128]{1,0:T(8,128)(2,1)S(1)}, bf16[528,128]{1,0:T(8,128)(2,1)S(1)}, u32[]{:S(2)}, u32[]{:S(2)}) collective-permute-start(bf16[528,128]{1,0:T(8,128)(2,1)S(1)} %get-tuple-element.67), channel_id=1, source_target_pairs={{0,8},{8,16},{16,24},{24,32},{32,40},{40,48},{48,56},{56,0},{1,9},... | collective-permute-start | bytes 405512 | tf_op jit(solution)/shard_map/ppermute | solution.py:29
  71.3 10.3 %collective-permute-start.13 = (bf16[528,128]{1,0:T(8,128)(2,1)S(1)}, bf16[528,128]{1,0:T(8,128)(2,1)S(1)}, u32[]{:S(2)}, u32[]{:S(2)}) collective-permute-start(bf16[528,128]{1,0:T(8,128)(2,1)S(1)} %get-tuple-element.69), channel_id=1, source_target_pairs={{0,16},{8,24},{16,32},{24,40},{32,48},{40,56},{48,0},{56,8},{1,17}... | collective-permute-start | bytes 405512 | tf_op jit(solution)/shard_map/ppermute | solution.py:29
  71.3 14.0 %collective-permute-start.16 = (bf16[528,128]{1,0:T(8,128)(2,1)S(1)}, bf16[528,128]{1,0:T(8,128)(2,1)S(1)}, u32[]{:S(2)}, u32[]{:S(2)}) collective-permute-start(bf16[528,128]{1,0:T(8,128)(2,1)S(1)} %get-tuple-element.71), channel_id=1, source_target_pairs={{0,56},{8,0},{16,8},{24,16},{32,24},{40,32},{48,40},{56,48},{1,57}... | collective-permute-start | bytes 405512 | tf_op jit(solution)/shard_map/ppermute | solution.py:29
  74.1 12.2 %collective-permute-start.20 = (bf16[512,128]{1,0:T(8,128)(2,1)S(1)}, bf16[512,128]{1,0:T(8,128)(2,1)S(1)}, u32[]{:S(2)}, u32[]{:S(2)}) collective-permute-start(bf16[512,128]{1,0:T(8,128)(2,1)S(1)} %add_convert_fusion.7), channel_id=1, source_target_pairs={{0,8},{8,16},{16,24},{24,32},{32,40},{40,48},{48,56},{56,0},{1,9},... | collective-permute-start | bytes 393224 | tf_op jit(solution)/shard_map/ppermute | solution.py:29
  74.3 18.6 %collective-permute-start.24 = (bf16[512,128]{1,0:T(8,128)(2,1)S(1)}, bf16[512,128]{1,0:T(8,128)(2,1)S(1)}, u32[]{:S(2)}, u32[]{:S(2)}) collective-permute-start(bf16[512,128]{1,0:T(8,128)(2,1)S(1)} %add_convert_fusion.5), channel_id=1, source_target_pairs={{0,56},{8,0},{16,8},{24,16},{32,24},{40,32},{48,40},{56,48},{1,57}... | collective-permute-start | bytes 393224 | tf_op jit(solution)/shard_map/ppermute | solution.py:29
  81.7 7.7 %collective-permute-start.14 = (bf16[528,128]{1,0:T(8,128)(2,1)S(1)}, bf16[528,128]{1,0:T(8,128)(2,1)S(1)}, u32[]{:S(2)}, u32[]{:S(2)}) collective-permute-start(bf16[528,128]{1,0:T(8,128)(2,1)S(1)} %add_convert_fusion.3), channel_id=1, source_target_pairs={{0,8},{8,16},{16,24},{24,32},{32,40},{40,48},{48,56},{56,0},{1,9},... | collective-permute-start | bytes 405512 | tf_op jit(solution)/shard_map/ppermute | solution.py:29
  85.4 6.4 %collective-permute-start.17 = (bf16[528,128]{1,0:T(8,128)(2,1)S(1)}, bf16[528,128]{1,0:T(8,128)(2,1)S(1)}, u32[]{:S(2)}, u32[]{:S(2)}) collective-permute-start(bf16[528,128]{1,0:T(8,128)(2,1)S(1)} %add_convert_fusion.1), channel_id=1, source_target_pairs={{0,56},{8,0},{16,8},{24,16},{32,24},{40,32},{48,40},{56,48},{1,57}... | collective-permute-start | bytes 405512 | tf_op jit(solution)/shard_map/ppermute | solution.py:29
  86.4 15.4 %collective-permute-start.21 = (bf16[512,128]{1,0:T(8,128)(2,1)S(1)}, bf16[512,128]{1,0:T(8,128)(2,1)S(1)}, u32[]{:S(2)}, u32[]{:S(2)}) collective-permute-start(bf16[512,128]{1,0:T(8,128)(2,1)S(1)} %add_convert_fusion.6), channel_id=1, source_target_pairs={{0,8},{8,16},{16,24},{24,32},{32,40},{40,48},{48,56},{56,0},{1,9},... | collective-permute-start | bytes 393224 | tf_op jit(solution)/shard_map/ppermute | solution.py:29
  89.4 6.3 %collective-permute-start.15 = (bf16[528,128]{1,0:T(8,128)(2,1)S(1)}, bf16[528,128]{1,0:T(8,128)(2,1)S(1)}, u32[]{:S(2)}, u32[]{:S(2)}) collective-permute-start(bf16[528,128]{1,0:T(8,128)(2,1)S(1)} %add_convert_fusion.2), channel_id=1, source_target_pairs={{0,8},{8,16},{16,24},{24,32},{32,40},{40,48},{48,56},{56,0},{1,9},... | collective-permute-start | bytes 405512 | tf_op jit(solution)/shard_map/ppermute | solution.py:29
  91.9 5.1 %collective-permute-start.18 = (bf16[528,128]{1,0:T(8,128)(2,1)S(1)}, bf16[528,128]{1,0:T(8,128)(2,1)S(1)}, u32[]{:S(2)}, u32[]{:S(2)}) collective-permute-start(bf16[528,128]{1,0:T(8,128)(2,1)S(1)} %add_convert_fusion), channel_id=1, source_target_pairs={{0,56},{8,0},{16,8},{24,16},{32,24},{40,32},{48,40},{56,48},{1,57}... | collective-permute-start | bytes 405512 | tf_op jit(solution)/shard_map/ppermute | solution.py:29
  92.9 8.8 %collective-permute-start.25 = (bf16[512,128]{1,0:T(8,128)(2,1)S(1)}, bf16[512,128]{1,0:T(8,128)(2,1)S(1)}, u32[]{:S(2)}, u32[]{:S(2)}) collective-permute-start(bf16[512,128]{1,0:T(8,128)(2,1)S(1)} %add_convert_fusion.4), channel_id=1, source_target_pairs={{0,56},{8,0},{16,8},{24,16},{32,24},{40,32},{48,40},{56,48},{1,57}... | collective-permute-start | bytes 393224 | tf_op jit(solution)/shard_map/ppermute | solution.py:29
  97.0 4.8 %collective-permute-start.28 = (bf16[16,128]{1,0:T(8,128)(2,1)S(1)}, bf16[16,128]{1,0:T(8,128)(2,1)S(1)}, u32[]{:S(2)}, u32[]{:S(2)}) collective-permute-start(bf16[16,128]{1,0:T(8,128)(2,1)S(1)} %add_convert_fusion.8.v0), channel_id=1, source_target_pairs={{0,192},{64,0},{128,64},{192,128},{1,193},{65,1},{129,65},{193,129... | collective-permute-start | bytes 12296 | tf_op jit(solution)/shard_map/ppermute | solution.py:29
  99.7 5.1 %collective-permute-start.27 = (bf16[16,128]{1,0:T(8,128)(2,1)S(1)}, bf16[16,128]{1,0:T(8,128)(2,1)S(1)}, u32[]{:S(2)}, u32[]{:S(2)}) collective-permute-start(bf16[16,128]{1,0:T(8,128)(2,1)S(1)} %add_convert_fusion.8.v0), channel_id=1, source_target_pairs={{0,128},{64,192},{128,0},{192,64},{1,129},{65,193},{129,1},{193,65... | collective-permute-start | bytes 12296 | tf_op jit(solution)/shard_map/ppermute | solution.py:29
  99.9 4.9 %collective-permute-start.26 = (bf16[16,128]{1,0:T(8,128)(2,1)S(1)}, bf16[16,128]{1,0:T(8,128)(2,1)S(1)}, u32[]{:S(2)}, u32[]{:S(2)}) collective-permute-start(bf16[16,128]{1,0:T(8,128)(2,1)S(1)} %add_convert_fusion.8.v0), channel_id=1, source_target_pairs={{0,64},{64,128},{128,192},{192,0},{1,65},{65,129},{129,193},{193,1... | collective-permute-start | bytes 12296 | tf_op jit(solution)/shard_map/ppermute | solution.py:29

commit v2 on v1

--- a/solution.py
+++ b/solution.py
@@ -19,7 +19,7 @@
 FIRST = 256
 CHUNKS = 2
 UNROLL = 32
-CUTS = 4
+CUTS = 16
 F32 = jnp.float32
 BF16 = jnp.bfloat16
 
@@ -33,19 +33,19 @@
     return pltpu.with_memory_space_constraint(array, pltpu.HBM)
 
 
-def dense_kernel(pos_ref, ids_ref, weights_ref, dense_ref, turned_ref, low_ref, key_ref, weight_ref):
+def dense_kernel(pos_ref, ids_ref, weights_ref, dense_ref, turned_ref, low_ref, key_ref, weight_ref, *, first):
     x, z, core = pos_ref[0], pos_ref[1], pos_ref[2]
-    terms, _ = ids_ref.shape
+    terms, queries = ids_ref.shape[0], dense_ref.shape[0]
     groups, pairs = low_ref.shape
     highs = dense_ref.shape[1] // FIRST
-    ids = ids_ref[...]
+    ids = ids_ref[:, first : first + queries]
     x_rel = ((ids >> 13) - x) & (NX - 1)
     half_rel = ((ids >> 9) & 1) ^ core
     high = x_rel * 4 + half_rel * 2 + ((ids >> 8) & 1)
     key = high * GROUP + (lax.broadcasted_iota(jnp.int32, ids.shape, 1) & (GROUP - 1))
     key = jnp.where(((ids >> 10) & (NZ - 1)) == z, key, -1)
     low = (ids & (FIRST - 1)).astype(F32)
-    weights = weights_ref[...].astype(F32)
+    weights = weights_ref[:, first : first + queries].astype(F32)
     turned_ref[...] = jnp.concatenate([low, key.astype(F32), weights, weights], axis=0).T
     place = lax.broadcasted_iota(jnp.int32, (groups, LANES), 1) // terms
     across = LANES // terms
@@ -82,13 +82,14 @@
     lax.fori_loop(0, groups // 2, pair_of_groups, 0, unroll=UNROLL)
 
 
-def build_dense(place, ids, weights, width):
-    terms, queries = ids.shape
+def build_dense(place, ids, weights, width, chunk):
+    terms = ids.shape[0]
+    queries = ids.shape[1] // CHUNKS
     groups = queries // GROUP
     rows = pltpu.VMEM((groups, GROUP * terms), F32)
     vmem = pl.BlockSpec(memory_space=pltpu.VMEM)
     return pl.pallas_call(
-        dense_kernel,
+        functools.partial(dense_kernel, first=chunk * queries),
         out_shape=pltpu.VMEM((queries, width), BF16),
         in_specs=[pl.BlockSpec(memory_space=pltpu.SMEM), vmem, vmem],
         out_specs=vmem,
@@ -135,7 +136,7 @@
 def score_kernel(pos_ref, impact_ref, dense_ref, *refs, extra, steps):
     piece_refs = refs[:6]
     extra_refs = refs[6:10] if extra else ()
-    out_refs = refs[-NZ - 3 : -3]
+    own_out, right_out, left_out, ahead_out, pair_right, pair_left = refs[-9:-3]
     made_ref, own_ref, own_sem = refs[-3:]
     x, z, core = pos_ref[0], pos_ref[1], pos_ref[2]
     depth, share = piece_refs[0].shape
@@ -166,6 +167,16 @@
             at = slice(step * rows, (step + 1) * rows)
             made_ref[2 * m, at, :] = jnp.where(left, a, pltpu.roll(b, half, 1)).astype(BF16)
             made_ref[2 * m + 1, at, :] = jnp.where(left, pltpu.roll(a, half, 1), b).astype(BF16)
+    out_refs = [
+        own_out,
+        pair_right.at[1],
+        right_out,
+        pair_right.at[0],
+        ahead_out,
+        pair_left.at[0],
+        left_out,
+        pair_left.at[1],
+    ]
     for j, out_ref in enumerate(out_refs):
         out_ref[:chunk, :] = made_ref[(z + j) & (NZ - 1)]
     if extra:
@@ -200,9 +211,10 @@
     hbm = pl.BlockSpec(memory_space=pltpu.HBM)
     return pl.pallas_call(
         functools.partial(score_kernel, extra=extra, steps=2),
-        out_shape=[jax.ShapeDtypeStruct((out_rows, LANES), BF16)] * NZ,
+        out_shape=[jax.ShapeDtypeStruct((out_rows, LANES), BF16)] * 4
+        + [jax.ShapeDtypeStruct((2, out_rows, LANES), BF16)] * 2,
         in_specs=[pl.BlockSpec(memory_space=pltpu.SMEM), hbm] + [vmem] * (1 + len(pieces) + len(more)),
-        out_specs=[vmem] * NZ,
+        out_specs=[vmem] * 6,
         scratch_shapes=[
             pltpu.VMEM((NZ, chunk, LANES), BF16),
             pltpu.VMEM((2, depth, share), BF16),
@@ -216,14 +228,17 @@
     )(place, kept_in_hbm(impact), dense, *pieces, *more)
 
 
-def cut_kernel(pos_ref, impact_ref, query_ref, named_ref, *refs, shifts):
-    rows_ref, out_refs, named_here, sem = refs[0], refs[1:-2], refs[-2], refs[-1]
+def cut_kernel(pos_ref, impact_ref, query_ref, named_ref, ids_ref, weights_ref, *refs, shifts):
+    rows_ref, ids_here, weights_here = refs[:3]
+    out_refs, named_here, sem = refs[3:-2], refs[-2], refs[-1]
     x, core = pos_ref[0], pos_ref[2]
     full, width = query_ref.shape
     count = len(out_refs) * CUTS
     copies = [
         pltpu.make_async_copy(named_ref, named_here, sem.at[count]),
         pltpu.make_async_copy(query_ref, rows_ref.at[:, pl.ds(0, width)], sem.at[count + 1]),
+        pltpu.make_async_copy(ids_ref, ids_here, sem.at[count + 2]),
+        pltpu.make_async_copy(weights_ref, weights_here, sem.at[count + 3]),
     ]
     for i, (out_ref, r) in enumerate(zip(out_refs, shifts)):
         depth, share = out_ref.shape
@@ -244,33 +259,40 @@
         copy.wait()
 
 
-def cut_slices(place, impact, query_rows, candidates, shifts):
+def cut_slices(place, impact, query_rows, candidates, ids, weights, shifts):
     full, width = query_rows.shape
     one = jax.ShapeDtypeStruct((impact.shape[0] // 2, impact.shape[1] // NX), BF16)
     vmem = pl.BlockSpec(memory_space=pltpu.VMEM)
     hbm = pl.BlockSpec(memory_space=pltpu.HBM)
-    rows, *cuts = pl.pallas_call(
+    rows, ids_here, weights_here, *cuts = pl.pallas_call(
         functools.partial(cut_kernel, shifts=shifts),
-        out_shape=[jax.ShapeDtypeStruct((full, width + LANES), BF16)] + [one] * len(shifts),
-        in_specs=[pl.BlockSpec(memory_space=pltpu.SMEM), hbm, hbm, hbm],
-        out_specs=[vmem] * (1 + len(shifts)),
+        out_shape=[
+            jax.ShapeDtypeStruct((full, width + LANES), BF16),
+            jax.ShapeDtypeStruct(ids.shape, ids.dtype),
+            jax.ShapeDtypeStruct(weights.shape, weights.dtype),
+        ]
+        + [one] * len(shifts),
+        in_specs=[pl.BlockSpec(memory_space=pltpu.SMEM)] + [hbm] * 5,
+        out_specs=[vmem] * (3 + len(shifts)),
         scratch_shapes=[
             pltpu.VMEM((CANDS, full), jnp.int32),
-            pltpu.SemaphoreType.DMA((len(shifts) * CUTS + 2,)),
+            pltpu.SemaphoreType.DMA((len(shifts) * CUTS + 4,)),
         ],
         compiler_params=pltpu.CompilerParams(vmem_limit_bytes=4 << 20),
         name="cut_slices",
-    )(place, kept_in_hbm(impact), kept_in_hbm(query_rows), kept_in_hbm(candidates.T))
-    return rows, cuts
-
-
-def final_kernel(pos_ref, a0, a1, a2, b0, b1, b2, v0, v1, v2, v3, first_ref, rescored_ref):
+    )(place, *[kept_in_hbm(a) for a in (impact, query_rows, candidates.T, ids, weights)])
+    return rows, ids_here, weights_here, cuts
+
+
+def final_kernel(pos_ref, *refs):
+    v0, v1, v2, v3, first_ref, rescored_ref = refs[10:]
     x = pos_ref[0]
     half = LANES // 2
-    chunk = b0.shape[0]
+    chunk = first_ref.shape[1] // 4
     column = 0
-    for own, one, two in ((a0, a1, a2), (b0, b1, b2)):
-        total = own[:chunk].astype(F32) + one[:chunk].astype(F32) + two[:chunk].astype(F32)
+    for own, right, left, far_right, far_left in (refs[:5], refs[5:10]):
+        total = own[:chunk].astype(F32) + right[1, :chunk].astype(F32) + left[1, :chunk].astype(F32)
+        total = total + far_right[:chunk].astype(F32) + far_left[:chunk].astype(F32)
         turned = total.T.astype(BF16)
         first_ref[:, column : column + chunk] = turned[:half]
         first_ref[:, column + chunk : column + 2 * chunk] = turned[half:]
@@ -285,7 +307,7 @@
 
 
 def finish(place, parts, sums, full):
-    chunk = parts[3].shape[0]
+    chunk = parts[5].shape[0]
     vmem = pl.BlockSpec(memory_space=pltpu.VMEM)
     return pl.pallas_call(
         final_kernel,
@@ -293,7 +315,7 @@
             jax.ShapeDtypeStruct((LANES // 2, 4 * chunk), BF16),
             jax.ShapeDtypeStruct((CANDS, LANES // (NX * NZ), full), F32),
         ],
-        in_specs=[pl.BlockSpec(memory_space=pltpu.SMEM)] + [vmem] * 10,
+        in_specs=[pl.BlockSpec(memory_space=pltpu.SMEM)] + [vmem] * 14,
         out_specs=[vmem] * 2,
         compiler_params=pltpu.CompilerParams(vmem_limit_bytes=8 << 20),
         name="finish",
@@ -311,35 +333,22 @@
     return lax.optimization_barrier((values, done))[0]
 
 
-def sent(values):
-    out = {}
-    for way in (1, -1):
-        out[way] = shifted(values[way], "z", way)
-    return out
+def passed(value, way):
+    return shifted(value, "z", way)
 
 
 def first_step(made, long_way):
-    ahead = shifted(made[4], "z", 2 * long_way)
-    return ahead, sent({1: made[3], -1: made[5]})
-
-
-def second_values(made, long_way, ahead, carried):
-    values = {1: [carried[1], made[2]], -1: [carried[-1], made[6]]}
+    ahead = passed(made[3], 2 * long_way)
+    return ahead, passed(made[4], 1), passed(made[5], -1)
+
+
+def second_step(made, long_way, going):
+    ahead, right, left = going
+    values = {1: [right[0], made[1]], -1: [left[0], made[2]]}
     values[long_way].append(ahead)
-    return {way: added(*parts) for way, parts in values.items()}
-
-
-def third_values(made, carried):
-    return {1: added(carried[1], made[1]), -1: added(carried[-1], made[7])}
-
-
-def rings(made_a, made_b, start_a, start_b):
-    (ahead_a, going_a), (ahead_b, going_b) = start_a, start_b
-    going_a = sent(second_values(made_a, 1, ahead_a, going_a))
-    going_b = sent(second_values(made_b, -1, ahead_b, going_b))
-    going_a = sent(third_values(made_a, going_a))
-    going_b = sent(third_values(made_b, going_b))
-    return (going_a[1], going_a[-1]), (going_b[1], going_b[-1])
+    far_right = passed(added(*values[1]), 2)
+    far_left = passed(added(*values[-1]), -2)
+    return made[0], right, left, far_right, far_left
 
 
 def scored(term_ids, term_weights, impact, query_rows, candidates):
@@ -352,20 +361,19 @@
     full = query_rows.shape[0]
 
     shifts = (1, 3, 2)
-    rows, cuts = cut_slices(place, impact, query_rows, candidates, shifts)
-    near = {r: shifted(one, "x", -r) for r, one in zip(shifts, cuts)}
-    (term_ids, term_weights), rows = lax.optimization_barrier(((term_ids, term_weights), rows))
-    gathered = [rows] + [shifted(rows, "prange", -r) for r in (1, 2, 3)]
-
-    ids = term_ids.T
-    weights = term_weights.T
-    half = ids.shape[1] // CHUNKS
-    dense_a = build_dense(place, ids[:, :half], weights[:, :half], NX * shard_width)
+    rows, ids, weights, cuts = cut_slices(place, impact, query_rows, candidates, term_ids.T, term_weights.T, shifts)
+    near = {}
+    for r, one in zip(shifts, cuts):
+        near[r] = shifted(one, "x", -r)
+    gathered = [rows]
+    for r in (1, 2, 3):
+        gathered.append(shifted(rows, "prange", -r))
+    dense_a = build_dense(place, ids, weights, NX * shard_width, 0)
     gathered = after(gathered, dense_a)
     by_home = score_rows(place, gathered, impact)
     back = [by_home[0]] + [shifted(by_home[r], "prange", r) for r in (1, 2, 3)]
     ids = after(ids, by_home)
-    dense_b = build_dense(place, ids[:, half:], weights[:, half:], NX * shard_width)
+    dense_b = build_dense(place, ids, weights, NX * shard_width, 1)
 
     near, back = after((near, back), dense_b)
     pieces = []
@@ -375,13 +383,15 @@
     start_a = first_step(made_a, 1)
     made_b = score_chunk(place, impact, dense_b, pieces, None)
     start_b = first_step(made_b, -1)
-    (a1, a2), (b1, b2) = rings(made_a, made_b, start_a, start_b)
+    parts_a = second_step(made_a, 1, start_a)
+    parts_b = second_step(made_b, -1, start_b)
     chunk = made_b[0].shape[0]
-    mine = added(made_a[0][chunk:], a1[chunk:], a2[chunk:])
+    mine = [part[1] if part.ndim == 3 else part for part in parts_a]
+    mine = added(*[part[chunk:] for part in mine])
     sums = [mine]
     for r in (1, 2, 3):
         sums.append(shifted(mine, "x", r))
-    first, rescored = finish(place, (made_a[0], a1, a2, made_b[0], b1, b2), sums, full)
+    first, rescored = finish(place, parts_a + parts_b, sums, full)
     return (first[None], jnp.transpose(rescored, (2, 0, 1)))
 
 

time: 107 us -> 109 us (1.019)
  the two profiles are of different devices: /device:TPU:2 before, /device:TPU:32 now
where the time goes in v2:
time: 109 us
  waiting for transfers between devices  40.4 us (37%)
  starting transfers between devices  35.5 us (33%)
  Pallas kernels  32.1 us (29%)
    ppermute x25, waiting for transfers between devices, shifted(): lax.ppermute(array, axis, [(i, (i + shift) % size) for i in range(size)])  40.4 us
    ppermute x25, starting transfers between devices, shifted(): lax.ppermute(array, axis, [(i, (i + shift) % size) for i in range(size)])  35.5 us
    pallas_call x2, Pallas kernels, build_dense(): pl.pallas_call(functools.partial(dense_kernel, first=chunk * queries), ou...  13.9 us
    pallas_call x2, Pallas kernels, score_chunk(): pl.pallas_call(functools.partial(score_kernel, extra=extra, steps=2), out...  12.8 us
    pallas_call x1, Pallas kernels, cut_slices(): pl.pallas_call(functools.partial(cut_kernel, shifts=shifts), out_shape=[j...  2.44 us
  transfers between devices with their start and end apart: 25, of which 12 were waited for; matrix products, arithmetic and copies ran while one was open for 0% of the time, Pallas kernels for 19%

profile of v2, /device:TPU:32, one launch (start us, length us, event | category | flops | bytes accessed | tf_op | source)
XLA Modules:
  0.0 109.0 jit_solution(13819969912694070672)
XLA Ops:
  0.6 0.1 pad_add_fusion.pos_ref
  0.7 2.4 %cut_slices.1 = (bf16[16,1152]{1,0:T(8,128)(2,1)S(1)}, s32[32,2048]{1,0:T(8,128)S(1)}, bf16[32,2048]{1,0:T(8,128)(2,1)S(1)}, bf16[512,512]{1,0:T(8,128)(2,1)S(1)...) custom-call(s32[4]{0:T(128)S(1)} %pad_add_fusion.pos_ref, bf16[1024,2048]{1,0:T(8,128)(2,1)} %impact_ref.7, ...), custom_call_target="tpu_custom_call" | custom-call | tf_op jit(solution)/shard_map/cut_slices/pallas_call | solution.py:267
  3.2 1.7 %collective-permute-start.5 = (bf16[16,1152]{1,0:T(8,128)(2,1)S(1)}, bf16[16,1152]{1,0:T(8,128)(2,1)S(1)}, u32[]{:S(2)}, u32[]{:S(2)}) collective-permute-start(bf16[16,1152]{1,0:T(8,128)(2,1)S(1)} %get-tuple-element.44.r0), channel_id=1, source_target_pairs={{0,2},{2,4},{4,6},{6,0},{1,3},{3,5},{5,7},{7,1},{8,10},{10,12},{12... | collective-permute-start | bytes 110600 | tf_op jit(solution)/shard_map/ppermute | solution.py:29
  4.8 2.9 %collective-permute-start.4 = (bf16[16,1152]{1,0:T(8,128)(2,1)S(1)}, bf16[16,1152]{1,0:T(8,128)(2,1)S(1)}, u32[]{:S(2)}, u32[]{:S(2)}) collective-permute-start(bf16[16,1152]{1,0:T(8,128)(2,1)S(1)} %get-tuple-element.44.r0), channel_id=1, source_target_pairs={{0,4},{2,6},{4,0},{6,2},{1,5},{3,7},{5,1},{7,3},{8,12},{10,14},{12... | collective-permute-start | bytes 110600 | tf_op jit(solution)/shard_map/ppermute | solution.py:29
  7.7 1.3 %collective-permute-start.3 = (bf16[16,1152]{1,0:T(8,128)(2,1)S(1)}, bf16[16,1152]{1,0:T(8,128)(2,1)S(1)}, u32[]{:S(2)}, u32[]{:S(2)}) collective-permute-start(bf16[16,1152]{1,0:T(8,128)(2,1)S(1)} %get-tuple-element.44.r0), channel_id=1, source_target_pairs={{0,6},{2,0},{4,2},{6,4},{1,7},{3,1},{5,3},{7,5},{8,14},{10,8},{12,... | collective-permute-start | bytes 110600 | tf_op jit(solution)/shard_map/ppermute | solution.py:29
  9.1 0.0 copy-start
  9.1 6.9 %dense_build.2.dense_ref = bf16[1024,4096]{1,0:T(8,128)(2,1)S(1)} custom-call(s32[4]{0:T(128)S(1)} %pad_add_fusion.pos_ref, s32[32,2048]{1,0:T(8,128)S(1)} %get-tuple-element.52.ids_ref, bf16[32,2048]{1,0:T(8,128)(2,1)S(1)} %get-tuple-element.39.weights_ref), custom_call_target="tpu_custom_call" | custom-call | flops 10000000000 | bytes 8388608 | tf_op jit(solution)/shard_map/dense_build/pallas_call | solution.py:91
  16.0 0.0 collective-permute-done.5.r3
  16.0 0.0 collective-permute-done.4.r2
  16.0 0.0 collective-permute-done.3.r1
  16.0 0.0 copy-done
  16.0 1.5 %score_rows.1 = (bf16[64,128]{1,0:T(8,128)(2,1)S(1)}, bf16[64,128]{1,0:T(8,128)(2,1)S(1)}, bf16[64,128]{1,0:T(8,128)(2,1)S(1)}, bf16[64,128]{1,0:T(8,128)(2,1)S(1)}) custom-call(s32[4]{0:T(128)S(1)} %pad_add_fusion.pos_ref, bf16[16,1152]{1,0:T(8,128)(2,1)S(1)} %get-tuple-element.44.r0, bf16[16,1152]{1,0:T(8,128)(2,1)S(1)} %collective-permute-done.3.r1, ...), custom_call_target="tpu_custom_call" | custom-call | flops 2000000000 | bytes 4194304 | tf_op jit(solution)/shard_map/score_rows/pallas_call | solution.py:125
  17.5 0.8 collective-permute-start.6
  18.3 2.7 %collective-permute-start = (bf16[512,512]{1,0:T(8,128)(2,1)S(1)}, bf16[512,512]{1,0:T(8,128)(2,1)S(1)}, u32[]{:S(2)}, u32[]{:S(2)}) collective-permute-start(bf16[512,512]{1,0:T(8,128)(2,1)S(1)} %get-tuple-element.40), channel_id=1, source_target_pairs={{0,192},{64,0},{128,64},{192,128},{1,193},{65,1},{129,65},{193,129... | collective-permute-start | bytes 1572872 | tf_op jit(solution)/shard_map/ppermute | solution.py:29
  21.0 0.8 collective-permute-start.1
  21.9 0.9 collective-permute-start.2
  22.7 0.8 collective-permute-start.7
  23.5 0.0 collective-permute-done.6.refs_7_
  23.5 2.0 %collective-permute-start.8 = (bf16[64,128]{1,0:T(8,128)(2,1)S(1)}, bf16[64,128]{1,0:T(8,128)(2,1)S(1)}, u32[]{:S(2)}, u32[]{:S(2)}) collective-permute-start(bf16[64,128]{1,0:T(8,128)(2,1)S(1)} %get-tuple-element.51), channel_id=1, source_target_pairs={{0,6},{2,0},{4,2},{6,4},{1,7},{3,1},{5,3},{7,5},{8,14},{10,8},{12,... | collective-permute-start | bytes 49160 | tf_op jit(solution)/shard_map/ppermute | solution.py:29
  25.5 6.9 %dense_build.3.dense_ref = bf16[1024,4096]{1,0:T(8,128)(2,1)S(1)} custom-call(s32[4]{0:T(128)S(1)} %pad_add_fusion.pos_ref, s32[32,2048]{1,0:T(8,128)S(1)} %get-tuple-element.52.ids_ref, bf16[32,2048]{1,0:T(8,128)(2,1)S(1)} %get-tuple-element.39.weights_ref), custom_call_target="tpu_custom_call" | custom-call | flops 10000000000 | bytes 8388608 | tf_op jit(solution)/shard_map/dense_build/pallas_call | solution.py:91
  32.4 0.0 collective-permute-done.7.refs_8_
  32.5 0.0 collective-permute-done.8.refs_9_
  32.5 9.9 %collective-permute-done.refs_0_ = bf16[512,512]{1,0:T(8,128)(2,1)S(1)} collective-permute-done((bf16[512,512]{1,0:T(8,128)(2,1)S(1)}, bf16[512,512]{1,0:T(8,128)(2,1)S(1)}, u32[]{:S(2)}, u32[]{:S(2)}) %collective-permute-start) | collective-permute-done | bytes 524320 | tf_op jit(solution)/shard_map/ppermute | solution.py:29
  42.4 0.0 collective-permute-done.1.refs_2_
  42.4 3.7 %collective-permute-done.2.refs_4_ = bf16[512,512]{1,0:T(8,128)(2,1)S(1)} collective-permute-done((bf16[512,512]{1,0:T(8,128)(2,1)S(1)}, bf16[512,512]{1,0:T(8,128)(2,1)S(1)}, u32[]{:S(2)}, u32[]{:S(2)}) %collective-permute-start.2) | collective-permute-done | bytes 524320 | tf_op jit(solution)/shard_map/ppermute | solution.py:29
  46.0 0.0 collective-permute-start.9
  46.1 0.5 collective-permute-start.10
  46.6 0.0 collective-permute-start.11
  46.6 1.4 %collective-permute-done.9.refs_1_ = bf16[512,512]{1,0:T(8,128)(2,1)S(1)} collective-permute-done((bf16[512,512]{1,0:T(8,128)(2,1)S(1)}, bf16[512,512]{1,0:T(8,128)(2,1)S(1)}, u32[]{:S(2)}, u32[]{:S(2)}) %collective-permute-start.9) | collective-permute-done | bytes 524320 | tf_op jit(solution)/shard_map/ppermute | solution.py:29
  48.0 0.7 collective-permute-done.10.refs_3_
  48.7 0.7 collective-permute-done.11.refs_5_
  49.5 6.3 %score_chunk.3 = (bf16[512,128]{1,0:T(8,128)(2,1)S(1)}, bf16[512,128]{1,0:T(8,128)(2,1)S(1)}, bf16[512,128]{1,0:T(8,128)(2,1)S(1)}, bf16[512,128]{1,0:T(8,128)(2...) custom-call(s32[4]{0:T(128)S(1)} %pad_add_fusion.pos_ref, bf16[1024,2048]{1,0:T(8,128)(2,1)} %impact_ref.7, ...), custom_call_target="tpu_custom_call" | custom-call | flops 4294967296 | bytes 8388608 | tf_op jit(solution)/shard_map/score_chunk/pallas_call | solution.py:212
  55.8 2.0 %collective-permute-start.17 = (bf16[2,512,128]{2,1,0:T(8,128)(2,1)S(1)}, bf16[2,512,128]{2,1,0:T(8,128)(2,1)S(1)}, u32[]{:S(2)}, u32[]{:S(2)}) collective-permute-start(bf16[2,512,128]{2,1,0:T(8,128)(2,1)S(1)} %get-tuple-element.67), channel_id=1, source_target_pairs={{0,8},{8,16},{16,24},{24,32},{32,40},{40,48},{48,56},{56,0},{1,9},... | collective-permute-start | bytes 786440 | tf_op jit(solution)/shard_map/ppermute | solution.py:29
  57.8 6.5 %score_chunk.2 = (bf16[528,128]{1,0:T(8,128)(2,1)S(1)}, bf16[528,128]{1,0:T(8,128)(2,1)S(1)}, bf16[528,128]{1,0:T(8,128)(2,1)S(1)}, bf16[528,128]{1,0:T(8,128)(2...) custom-call(s32[4]{0:T(128)S(1)} %pad_add_fusion.pos_ref, bf16[1024,2048]{1,0:T(8,128)(2,1)} %impact_ref.7, ...), custom_call_target="tpu_custom_call" | custom-call | flops 4294967296 | bytes 8388608 | tf_op jit(solution)/shard_map/score_chunk/pallas_call | solution.py:212
  64.3 2.2 %collective-permute-start.12 = (bf16[2,528,128]{2,1,0:T(8,128)(2,1)S(1)}, bf16[2,528,128]{2,1,0:T(8,128)(2,1)S(1)}, u32[]{:S(2)}, u32[]{:S(2)}) collective-permute-start(bf16[2,528,128]{2,1,0:T(8,128)(2,1)S(1)} %get-tuple-element.61), channel_id=1, source_target_pairs={{0,8},{8,16},{16,24},{24,32},{32,40},{40,48},{48,56},{56,0},{1,9},... | collective-permute-start | bytes 811016 | tf_op jit(solution)/shard_map/ppermute | solution.py:29
  66.5 1.7 %collective-permute-start.20 = (bf16[512,128]{1,0:T(8,128)(2,1)S(1)}, bf16[512,128]{1,0:T(8,128)(2,1)S(1)}, u32[]{:S(2)}, u32[]{:S(2)}) collective-permute-start(bf16[512,128]{1,0:T(8,128)(2,1)S(1)} %get-tuple-element.71), channel_id=1, source_target_pairs={{0,48},{8,56},{16,0},{24,8},{32,16},{40,24},{48,32},{56,40},{1,49}... | collective-permute-start | bytes 393224 | tf_op jit(solution)/shard_map/ppermute | solution.py:29
  68.2 1.9 %collective-permute-start.14 = (bf16[528,128]{1,0:T(8,128)(2,1)S(1)}, bf16[528,128]{1,0:T(8,128)(2,1)S(1)}, u32[]{:S(2)}, u32[]{:S(2)}) collective-permute-start(bf16[528,128]{1,0:T(8,128)(2,1)S(1)} %get-tuple-element.64), channel_id=1, source_target_pairs={{0,16},{8,24},{16,32},{24,40},{32,48},{40,56},{48,0},{56,8},{1,17}... | collective-permute-start | bytes 405512 | tf_op jit(solution)/shard_map/ppermute | solution.py:29
  70.1 1.0 collective-permute-start.18
  71.1 0.0 collective-permute-done.17.refs_6_
  71.1 1.8 %collective-permute-start.13 = (bf16[2,528,128]{2,1,0:T(8,128)(2,1)S(1)}, bf16[2,528,128]{2,1,0:T(8,128)(2,1)S(1)}, u32[]{:S(2)}, u32[]{:S(2)}) collective-permute-start(bf16[2,528,128]{2,1,0:T(8,128)(2,1)S(1)} %get-tuple-element.62), channel_id=1, source_target_pairs={{0,56},{8,0},{16,8},{24,16},{32,24},{40,32},{48,40},{56,48},{1,57}... | collective-permute-start | bytes 811016 | tf_op jit(solution)/shard_map/ppermute | solution.py:29
  72.9 7.7 %collective-permute-done.14 = bf16[528,128]{1,0:T(8,128)(2,1)S(1)} collective-permute-done((bf16[528,128]{1,0:T(8,128)(2,1)S(1)}, bf16[528,128]{1,0:T(8,128)(2,1)S(1)}, u32[]{:S(2)}, u32[]{:S(2)}) %collective-permute-start.14) | collective-permute-done | bytes 135200 | tf_op jit(solution)/shard_map/ppermute | solution.py:29
  80.7 0.8 collective-permute-start.19
  81.5 0.0 collective-permute-done.12.refs_1_
  81.5 0.1 fusion.2
  81.6 3.2 %collective-permute-start.15 = (bf16[528,128]{1,0:T(8,128)(2,1)S(1)}, bf16[528,128]{1,0:T(8,128)(2,1)S(1)}, u32[]{:S(2)}, u32[]{:S(2)}) collective-permute-start(bf16[528,128]{1,0:T(8,128)(2,1)S(1)} %fusion.2), channel_id=1, source_target_pairs={{0,16},{8,24},{16,32},{24,40},{32,48},{40,56},{48,0},{56,8},{1,17}... | collective-permute-start | bytes 405512 | tf_op jit(solution)/shard_map/ppermute | solution.py:29
  84.8 2.4 %collective-permute-done.13.refs_2_ = bf16[2,528,128]{2,1,0:T(8,128)(2,1)S(1)} collective-permute-done((bf16[2,528,128]{2,1,0:T(8,128)(2,1)S(1)}, bf16[2,528,128]{2,1,0:T(8,128)(2,1)S(1)}, u32[]{:S(2)}, u32[]{:S(2)}) %collective-permute-start.13) | collective-permute-done | bytes 270368 | tf_op jit(solution)/shard_map/ppermute | solution.py:29
  87.2 3.0 %collective-permute-start.16 = (bf16[528,128]{1,0:T(8,128)(2,1)S(1)}, bf16[528,128]{1,0:T(8,128)(2,1)S(1)}, u32[]{:S(2)}, u32[]{:S(2)}) collective-permute-start(bf16[528,128]{1,0:T(8,128)(2,1)S(1)} %fusion), channel_id=1, source_target_pairs={{0,48},{8,56},{16,0},{24,8},{32,16},{40,24},{48,32},{56,40},{1,49}... | collective-permute-start | bytes 405512 | tf_op jit(solution)/shard_map/ppermute | solution.py:29
  90.2 0.0 collective-permute-done.20
  90.2 0.0 collective-permute-done.18.refs_7_
  90.2 0.1 fusion.4
  90.2 1.3 %collective-permute-start.21 = (bf16[512,128]{1,0:T(8,128)(2,1)S(1)}, bf16[512,128]{1,0:T(8,128)(2,1)S(1)}, u32[]{:S(2)}, u32[]{:S(2)}) collective-permute-start(bf16[512,128]{1,0:T(8,128)(2,1)S(1)} %fusion.4), channel_id=1, source_target_pairs={{0,48},{8,56},{16,0},{24,8},{32,16},{40,24},{48,32},{56,40},{1,49}... | collective-permute-start | bytes 393224 | tf_op jit(solution)/shard_map/ppermute | solution.py:29
  91.5 2.6 %collective-permute-done.15.refs_3_ = bf16[528,128]{1,0:T(8,128)(2,1)S(1)} collective-permute-done((bf16[528,128]{1,0:T(8,128)(2,1)S(1)}, bf16[528,128]{1,0:T(8,128)(2,1)S(1)}, u32[]{:S(2)}, u32[]{:S(2)}) %collective-permute-start.15) | collective-permute-done | bytes 135200 | tf_op jit(solution)/shard_map/ppermute | solution.py:29
  94.1 7.1 %collective-permute-done.16.refs_4_ = bf16[528,128]{1,0:T(8,128)(2,1)S(1)} collective-permute-done((bf16[528,128]{1,0:T(8,128)(2,1)S(1)}, bf16[528,128]{1,0:T(8,128)(2,1)S(1)}, u32[]{:S(2)}, u32[]{:S(2)}) %collective-permute-start.16) | collective-permute-done | bytes 135200 | tf_op jit(solution)/shard_map/ppermute | solution.py:29
  101.2 0.6 collective-permute-start.24
  101.8 0.8 collective-permute-start.23
  102.6 0.8 collective-permute-start.22
  103.4 0.0 collective-permute-done.19.refs_8_
  103.4 0.0 collective-permute-done.21.refs_9_
  103.4 1.4 %collective-permute-done.24.refs_13_ = bf16[16,128]{1,0:T(8,128)(2,1)S(1)} collective-permute-done((bf16[16,128]{1,0:T(8,128)(2,1)S(1)}, bf16[16,128]{1,0:T(8,128)(2,1)S(1)}, u32[]{:S(2)}, u32[]{:S(2)}) %collective-permute-start.24) | collective-permute-done | bytes 4128 | tf_op jit(solution)/shard_map/ppermute | solution.py:29
  104.8 2.1 %collective-permute-done.23.refs_12_ = bf16[16,128]{1,0:T(8,128)(2,1)S(1)} collective-permute-done((bf16[16,128]{1,0:T(8,128)(2,1)S(1)}, bf16[16,128]{1,0:T(8,128)(2,1)S(1)}, u32[]{:S(2)}, u32[]{:S(2)}) %collective-permute-start.23) | collective-permute-done | bytes 4128 | tf_op jit(solution)/shard_map/ppermute | solution.py:29
  106.9 0.6 collective-permute-done.22.refs_11_
  107.5 1.5 %finish.1 = (bf16[64,2048]{1,0:T(8,128)(2,1)}, f32[4,4,16]{2,1,0:T(4,128)}) custom-call(s32[4]{0:T(128)S(1)} %pad_add_fusion.pos_ref, bf16[528,128]{1,0:T(8,128)(2,1)S(1)} %get-tuple-element.60.refs_0_, bf16[2,528,128]{2,1,0:T(8,128)(2,1)S(1)} %collective-permute-done.12.refs_1_, bf16[2,528,128]{2,1,0:T(8,128)(2,1)S(1)} %collective-permute-done.13.refs_2_, ...), custom_call_target="tpu_custom_call" | custom-call | tf_op jit(solution)/shard_map/finish/pallas_call | solution.py:312
  (3 shorter events, 0.1 us)
Async XLA Ops:
  3.2 12.8 %collective-permute-start.5 = (bf16[16,1152]{1,0:T(8,128)(2,1)S(1)}, bf16[16,1152]{1,0:T(8,128)(2,1)S(1)}, u32[]{:S(2)}, u32[]{:S(2)}) collective-permute-start(bf16[16,1152]{1,0:T(8,128)(2,1)S(1)} %get-tuple-element.44.r0), channel_id=1, source_target_pairs={{0,2},{2,4},{4,6},{6,0},{1,3},{3,5},{5,7},{7,1},{8,10},{10,12},{12... | collective-permute-start | bytes 110600 | tf_op jit(solution)/shard_map/ppermute | solution.py:29
  4.8 11.2 %collective-permute-start.4 = (bf16[16,1152]{1,0:T(8,128)(2,1)S(1)}, bf16[16,1152]{1,0:T(8,128)(2,1)S(1)}, u32[]{:S(2)}, u32[]{:S(2)}) collective-permute-start(bf16[16,1152]{1,0:T(8,128)(2,1)S(1)} %get-tuple-element.44.r0), channel_id=1, source_target_pairs={{0,4},{2,6},{4,0},{6,2},{1,5},{3,7},{5,1},{7,3},{8,12},{10,14},{12... | collective-permute-start | bytes 110600 | tf_op jit(solution)/shard_map/ppermute | solution.py:29
  7.7 8.3 %collective-permute-start.3 = (bf16[16,1152]{1,0:T(8,128)(2,1)S(1)}, bf16[16,1152]{1,0:T(8,128)(2,1)S(1)}, u32[]{:S(2)}, u32[]{:S(2)}) collective-permute-start(bf16[16,1152]{1,0:T(8,128)(2,1)S(1)} %get-tuple-element.44.r0), channel_id=1, source_target_pairs={{0,6},{2,0},{4,2},{6,4},{1,7},{3,1},{5,3},{7,5},{8,14},{10,8},{12,... | collective-permute-start | bytes 110600 | tf_op jit(solution)/shard_map/ppermute | solution.py:29
  9.1 7.0 %copy-start = (bf16[1024,2048]{1,0:T(8,128)(2,1)S(1)}, bf16[1024,2048]{1,0:T(8,128)(2,1)}, u32[]{:S(2)}) copy-start(bf16[1024,2048]{1,0:T(8,128)(2,1)} %impact_ref.7) | copy-start | bytes 12582916
  17.5 6.0 %collective-permute-start.6 = (bf16[64,128]{1,0:T(8,128)(2,1)S(1)}, bf16[64,128]{1,0:T(8,128)(2,1)S(1)}, u32[]{:S(2)}, u32[]{:S(2)}) collective-permute-start(bf16[64,128]{1,0:T(8,128)(2,1)S(1)} %get-tuple-element.49), channel_id=1, source_target_pairs={{0,2},{2,4},{4,6},{6,0},{1,3},{3,5},{5,7},{7,1},{8,10},{10,12},{12... | collective-permute-start | bytes 49160 | tf_op jit(solution)/shard_map/ppermute | solution.py:29
  18.3 24.1 %collective-permute-start = (bf16[512,512]{1,0:T(8,128)(2,1)S(1)}, bf16[512,512]{1,0:T(8,128)(2,1)S(1)}, u32[]{:S(2)}, u32[]{:S(2)}) collective-permute-start(bf16[512,512]{1,0:T(8,128)(2,1)S(1)} %get-tuple-element.40), channel_id=1, source_target_pairs={{0,192},{64,0},{128,64},{192,128},{1,193},{65,1},{129,65},{193,129... | collective-permute-start | bytes 1572872 | tf_op jit(solution)/shard_map/ppermute | solution.py:29
  21.0 21.3 %collective-permute-start.1 = (bf16[512,512]{1,0:T(8,128)(2,1)S(1)}, bf16[512,512]{1,0:T(8,128)(2,1)S(1)}, u32[]{:S(2)}, u32[]{:S(2)}) collective-permute-start(bf16[512,512]{1,0:T(8,128)(2,1)S(1)} %get-tuple-element.41), channel_id=1, source_target_pairs={{0,128},{64,192},{128,0},{192,64},{1,129},{65,193},{129,1},{193,65... | collective-permute-start | bytes 1572872 | tf_op jit(solution)/shard_map/ppermute | solution.py:29
  21.9 24.2 %collective-permute-start.2 = (bf16[512,512]{1,0:T(8,128)(2,1)S(1)}, bf16[512,512]{1,0:T(8,128)(2,1)S(1)}, u32[]{:S(2)}, u32[]{:S(2)}) collective-permute-start(bf16[512,512]{1,0:T(8,128)(2,1)S(1)} %get-tuple-element.42), channel_id=1, source_target_pairs={{0,64},{64,128},{128,192},{192,0},{1,65},{65,129},{129,193},{193,1... | collective-permute-start | bytes 1572872 | tf_op jit(solution)/shard_map/ppermute | solution.py:29
  22.7 9.7 %collective-permute-start.7 = (bf16[64,128]{1,0:T(8,128)(2,1)S(1)}, bf16[64,128]{1,0:T(8,128)(2,1)S(1)}, u32[]{:S(2)}, u32[]{:S(2)}) collective-permute-start(bf16[64,128]{1,0:T(8,128)(2,1)S(1)} %get-tuple-element.50), channel_id=1, source_target_pairs={{0,4},{2,6},{4,0},{6,2},{1,5},{3,7},{5,1},{7,3},{8,12},{10,14},{12... | collective-permute-start | bytes 49160 | tf_op jit(solution)/shard_map/ppermute | solution.py:29
  23.5 8.9 %collective-permute-start.8 = (bf16[64,128]{1,0:T(8,128)(2,1)S(1)}, bf16[64,128]{1,0:T(8,128)(2,1)S(1)}, u32[]{:S(2)}, u32[]{:S(2)}) collective-permute-start(bf16[64,128]{1,0:T(8,128)(2,1)S(1)} %get-tuple-element.51), channel_id=1, source_target_pairs={{0,6},{2,0},{4,2},{6,4},{1,7},{3,1},{5,3},{7,5},{8,14},{10,8},{12,... | collective-permute-start | bytes 49160 | tf_op jit(solution)/shard_map/ppermute | solution.py:29
  46.0 1.9 %collective-permute-start.9 = (bf16[512,512]{1,0:T(8,128)(2,1)S(1)}, bf16[512,512]{1,0:T(8,128)(2,1)S(1)}, u32[]{:S(2)}, u32[]{:S(2)}) collective-permute-start(bf16[512,512]{1,0:T(8,128)(2,1)S(1)} %collective-permute-done.refs_0_), channel_id=1, source_target_pairs={{0,1},{1,0},{2,3},{3,2},{4,5},{5,4},{6,7},{7,6},{8,9},{9,8},{10,11... | collective-permute-start | bytes 1572872 | tf_op jit(solution)/shard_map/ppermute | solution.py:29
  46.1 2.6 %collective-permute-start.10 = (bf16[512,512]{1,0:T(8,128)(2,1)S(1)}, bf16[512,512]{1,0:T(8,128)(2,1)S(1)}, u32[]{:S(2)}, u32[]{:S(2)}) collective-permute-start(bf16[512,512]{1,0:T(8,128)(2,1)S(1)} %collective-permute-done.1.refs_2_), channel_id=1, source_target_pairs={{0,1},{1,0},{2,3},{3,2},{4,5},{5,4},{6,7},{7,6},{8,9},{9,8},{10,11... | collective-permute-start | bytes 1572872 | tf_op jit(solution)/shard_map/ppermute | solution.py:29
  46.6 2.9 %collective-permute-start.11 = (bf16[512,512]{1,0:T(8,128)(2,1)S(1)}, bf16[512,512]{1,0:T(8,128)(2,1)S(1)}, u32[]{:S(2)}, u32[]{:S(2)}) collective-permute-start(bf16[512,512]{1,0:T(8,128)(2,1)S(1)} %collective-permute-done.2.refs_4_), channel_id=1, source_target_pairs={{0,1},{1,0},{2,3},{3,2},{4,5},{5,4},{6,7},{7,6},{8,9},{9,8},{10,11... | collective-permute-start | bytes 1572872 | tf_op jit(solution)/shard_map/ppermute | solution.py:29
  55.8 15.3 %collective-permute-start.17 = (bf16[2,512,128]{2,1,0:T(8,128)(2,1)S(1)}, bf16[2,512,128]{2,1,0:T(8,128)(2,1)S(1)}, u32[]{:S(2)}, u32[]{:S(2)}) collective-permute-start(bf16[2,512,128]{2,1,0:T(8,128)(2,1)S(1)} %get-tuple-element.67), channel_id=1, source_target_pairs={{0,8},{8,16},{16,24},{24,32},{32,40},{40,48},{48,56},{56,0},{1,9},... | collective-permute-start | bytes 786440 | tf_op jit(solution)/shard_map/ppermute | solution.py:29
  64.3 17.2 %collective-permute-start.12 = (bf16[2,528,128]{2,1,0:T(8,128)(2,1)S(1)}, bf16[2,528,128]{2,1,0:T(8,128)(2,1)S(1)}, u32[]{:S(2)}, u32[]{:S(2)}) collective-permute-start(bf16[2,528,128]{2,1,0:T(8,128)(2,1)S(1)} %get-tuple-element.61), channel_id=1, source_target_pairs={{0,8},{8,16},{16,24},{24,32},{32,40},{40,48},{48,56},{56,0},{1,9},... | collective-permute-start | bytes 811016 | tf_op jit(solution)/shard_map/ppermute | solution.py:29
  66.5 23.7 %collective-permute-start.20 = (bf16[512,128]{1,0:T(8,128)(2,1)S(1)}, bf16[512,128]{1,0:T(8,128)(2,1)S(1)}, u32[]{:S(2)}, u32[]{:S(2)}) collective-permute-start(bf16[512,128]{1,0:T(8,128)(2,1)S(1)} %get-tuple-element.71), channel_id=1, source_target_pairs={{0,48},{8,56},{16,0},{24,8},{32,16},{40,24},{48,32},{56,40},{1,49}... | collective-permute-start | bytes 393224 | tf_op jit(solution)/shard_map/ppermute | solution.py:29
  68.2 12.5 %collective-permute-start.14 = (bf16[528,128]{1,0:T(8,128)(2,1)S(1)}, bf16[528,128]{1,0:T(8,128)(2,1)S(1)}, u32[]{:S(2)}, u32[]{:S(2)}) collective-permute-start(bf16[528,128]{1,0:T(8,128)(2,1)S(1)} %get-tuple-element.64), channel_id=1, source_target_pairs={{0,16},{8,24},{16,32},{24,40},{32,48},{40,56},{48,0},{56,8},{1,17}... | collective-permute-start | bytes 405512 | tf_op jit(solution)/shard_map/ppermute | solution.py:29
  70.1 20.1 %collective-permute-start.18 = (bf16[2,512,128]{2,1,0:T(8,128)(2,1)S(1)}, bf16[2,512,128]{2,1,0:T(8,128)(2,1)S(1)}, u32[]{:S(2)}, u32[]{:S(2)}) collective-permute-start(bf16[2,512,128]{2,1,0:T(8,128)(2,1)S(1)} %get-tuple-element.68), channel_id=1, source_target_pairs={{0,56},{8,0},{16,8},{24,16},{32,24},{40,32},{48,40},{56,48},{1,57}... | collective-permute-start | bytes 786440 | tf_op jit(solution)/shard_map/ppermute | solution.py:29
  71.1 16.0 %collective-permute-start.13 = (bf16[2,528,128]{2,1,0:T(8,128)(2,1)S(1)}, bf16[2,528,128]{2,1,0:T(8,128)(2,1)S(1)}, u32[]{:S(2)}, u32[]{:S(2)}) collective-permute-start(bf16[2,528,128]{2,1,0:T(8,128)(2,1)S(1)} %get-tuple-element.62), channel_id=1, source_target_pairs={{0,56},{8,0},{16,8},{24,16},{32,24},{40,32},{48,40},{56,48},{1,57}... | collective-permute-start | bytes 811016 | tf_op jit(solution)/shard_map/ppermute | solution.py:29
  80.7 22.8 %collective-permute-start.19 = (bf16[512,128]{1,0:T(8,128)(2,1)S(1)}, bf16[512,128]{1,0:T(8,128)(2,1)S(1)}, u32[]{:S(2)}, u32[]{:S(2)}) collective-permute-start(bf16[512,128]{1,0:T(8,128)(2,1)S(1)} %fusion.5), channel_id=1, source_target_pairs={{0,16},{8,24},{16,32},{24,40},{32,48},{40,56},{48,0},{56,8},{1,17}... | collective-permute-start | bytes 393224 | tf_op jit(solution)/shard_map/ppermute | solution.py:29
  81.6 12.6 %collective-permute-start.15 = (bf16[528,128]{1,0:T(8,128)(2,1)S(1)}, bf16[528,128]{1,0:T(8,128)(2,1)S(1)}, u32[]{:S(2)}, u32[]{:S(2)}) collective-permute-start(bf16[528,128]{1,0:T(8,128)(2,1)S(1)} %fusion.2), channel_id=1, source_target_pairs={{0,16},{8,24},{16,32},{24,40},{32,48},{40,56},{48,0},{56,8},{1,17}... | collective-permute-start | bytes 405512 | tf_op jit(solution)/shard_map/ppermute | solution.py:29
  87.2 14.0 %collective-permute-start.16 = (bf16[528,128]{1,0:T(8,128)(2,1)S(1)}, bf16[528,128]{1,0:T(8,128)(2,1)S(1)}, u32[]{:S(2)}, u32[]{:S(2)}) collective-permute-start(bf16[528,128]{1,0:T(8,128)(2,1)S(1)} %fusion), channel_id=1, source_target_pairs={{0,48},{8,56},{16,0},{24,8},{32,16},{40,24},{48,32},{56,40},{1,49}... | collective-permute-start | bytes 405512 | tf_op jit(solution)/shard_map/ppermute | solution.py:29
  90.2 13.2 %collective-permute-start.21 = (bf16[512,128]{1,0:T(8,128)(2,1)S(1)}, bf16[512,128]{1,0:T(8,128)(2,1)S(1)}, u32[]{:S(2)}, u32[]{:S(2)}) collective-permute-start(bf16[512,128]{1,0:T(8,128)(2,1)S(1)} %fusion.4), channel_id=1, source_target_pairs={{0,48},{8,56},{16,0},{24,8},{32,16},{40,24},{48,32},{56,40},{1,49}... | collective-permute-start | bytes 393224 | tf_op jit(solution)/shard_map/ppermute | solution.py:29
  101.2 3.6 %collective-permute-start.24 = (bf16[16,128]{1,0:T(8,128)(2,1)S(1)}, bf16[16,128]{1,0:T(8,128)(2,1)S(1)}, u32[]{:S(2)}, u32[]{:S(2)}) collective-permute-start(bf16[16,128]{1,0:T(8,128)(2,1)S(1)} %fusion.8.refs_10_), channel_id=1, source_target_pairs={{0,192},{64,0},{128,64},{192,128},{1,193},{65,1},{129,65},{193,129... | collective-permute-start | bytes 12296 | tf_op jit(solution)/shard_map/ppermute | solution.py:29
  101.8 5.1 %collective-permute-start.23 = (bf16[16,128]{1,0:T(8,128)(2,1)S(1)}, bf16[16,128]{1,0:T(8,128)(2,1)S(1)}, u32[]{:S(2)}, u32[]{:S(2)}) collective-permute-start(bf16[16,128]{1,0:T(8,128)(2,1)S(1)} %fusion.8.refs_10_), channel_id=1, source_target_pairs={{0,128},{64,192},{128,0},{192,64},{1,129},{65,193},{129,1},{193,65... | collective-permute-start | bytes 12296 | tf_op jit(solution)/shard_map/ppermute | solution.py:29
  102.6 4.9 %collective-permute-start.22 = (bf16[16,128]{1,0:T(8,128)(2,1)S(1)}, bf16[16,128]{1,0:T(8,128)(2,1)S(1)}, u32[]{:S(2)}, u32[]{:S(2)}) collective-permute-start(bf16[16,128]{1,0:T(8,128)(2,1)S(1)} %fusion.8.refs_10_), channel_id=1, source_target_pairs={{0,64},{64,128},{128,192},{192,0},{1,65},{65,129},{129,193},{193,1... | collective-permute-start | bytes 12296 | tf_op jit(solution)/shard_map/ppermute | solution.py:29
